TPU v7x, 32 devices: a whole 2x2x4 slice. The times are simulated.
32 devices in a mesh: groups: 2 (over x), seq: 16 (over z, y, core).
Axes of the slice: x: 2, y: 2, z: 4, core: 2. Of those that a mesh axis runs over, the one named last changes fastest.
Arguments:
- prefill_q: bfloat16 [32, 8192], P(('groups', 'seq')), parts along dimension 0, may hold values from -48 to 48
- cache_k: bfloat16 [16384, 1024], P(('groups', 'seq')), parts along dimension 0, may hold values from -4.5 to 4.5
- cache_v: bfloat16 [16384, 1024], P(('groups', 'seq')), parts along dimension 0, may hold values from -4.5 to 4.5
- page_counts: int32 [32], P('groups'), parts along dimension 0, may hold values from 1 to 64, 768 in all
- page_owner: int32 [2048, 1], P(('groups', 'seq')), parts along dimension 0, may hold values from 0 to 15; in each aligned block of 64 rows (0 to 63, 64 to 127, ...) at most 8 rows name the same one
- decode_q: bfloat16 [32, 2, 8192], P(('groups', 'seq')), parts along dimension 0, may hold values from -48 to 48
- decode_k: bfloat16 [32, 2, 1024], P(('groups', 'seq')), parts along dimension 0, may hold values from -12 to 12
- decode_v: bfloat16 [32, 2, 1024], P(('groups', 'seq')), parts along dimension 0, may hold values from -4.5 to 4.5
- context_len: int32 [32], P(('groups', 'seq')), parts along dimension 0, may hold values from 768 to 6144
Outputs:
- prefill_out: bfloat16 [32, 8192], P(('groups', 'seq')), parts along dimension 0
- decode_out: bfloat16 [32, 2, 8192], P(('groups', 'seq')), parts along dimension 0
- store_k: bfloat16 [32768, 1024], P(('groups', 'seq')), parts along dimension 0
- store_v: bfloat16 [32768, 1024], P(('groups', 'seq')), parts along dimension 0
- store_page: int32 [4096], P(('groups', 'seq')), parts along dimension 0
There are 2 independent parts, one for each index of `groups`. A program takes and returns all parts, laid end to end along the dimension named above; each array names one. Nothing has to cross between parts.
Inputs may be any that keep to these rules, and one draw needn't show every extreme that they name: `page_counts`: the counts sum to 768 and the largest equals 64. `page_owner`: within the 64 page slots of one shard each owner is named at most 8 times, and exactly 8 times in some shards.
All inputs are finite; a program needn't handle non-finite values.
Results may differ from a plain program's by a relative error of at most 0.014.
Values may be sent and summed in bfloat16 or wider, within the bound.
A program may use at most 128 MiB of HBM per device.

v0:
```python
import jax
import jax.numpy as jnp
from jax import lax
from jax.sharding import PartitionSpec as P

HQ = 64
KVH = 8
HD = 128
PAGE = 8
STEPS = 2
KVD = 1024


MASKED = -1e30


def partial_attend(queries, key_block, value_block, allowed):
    height = queries.shape[0]
    grouping = HQ // KVH
    scaling = HD ** (-0.5)
    start_state = (
        jnp.zeros((height, HQ * HD), jnp.float32),
        jnp.zeros((height, HQ), jnp.float32),
        jnp.zeros((height, HQ), jnp.float32),
    )

    def one_group(member, state):
        weighted, highs, totals = state
        query_group = lax.dynamic_slice_in_dim(
            queries, member * grouping * HD, grouping * HD, 1
        ).reshape(height, grouping, HD)
        key_group = lax.dynamic_slice_in_dim(key_block, member * HD, HD, 1)
        value_group = lax.dynamic_slice_in_dim(value_block, member * HD, HD, 1)
        scores = (
            jnp.einsum("qhd,kd->qhk", query_group, key_group, preferred_element_type=jnp.float32)
            * scaling
        )
        scores = jnp.where(allowed[:, None, :], scores, MASKED)
        highest = jnp.max(scores, axis=2)
        weights = jnp.where(allowed[:, None, :], jnp.exp(scores - highest[:, :, None]), 0.0)
        summed = jnp.sum(weights, axis=2)
        product = jnp.einsum(
            "qhk,kd->qhd",
            weights.astype(jnp.bfloat16),
            value_group,
            preferred_element_type=jnp.float32,
        )
        weighted = lax.dynamic_update_slice_in_dim(
            weighted, product.reshape(height, grouping * HD), member * grouping * HD, 1
        )
        highs = lax.dynamic_update_slice_in_dim(highs, highest, member * grouping, 1)
        totals = lax.dynamic_update_slice_in_dim(totals, summed, member * grouping, 1)
        return (weighted, highs, totals)

    return lax.fori_loop(0, KVH, one_group, start_state)


def combine_parts(pieces):
    weighted, highs, totals = pieces
    sources = highs.shape[0]
    height = highs.shape[1]
    highest = jnp.max(highs, axis=0)
    factor = jnp.exp(highs - highest[None])
    totals = jnp.sum(factor * totals, axis=0)
    weighted = jnp.sum(weighted.reshape(sources, height, HQ, HD) * factor[:, :, :, None], axis=0)
    return (weighted.reshape(height, HQ * HD), highest, totals)


def per_device(
    prefill_q, cache_k, cache_v, page_counts, page_owner, decode_q, decode_k, decode_v, context_len
):
    shards = lax.axis_size("seq")
    myself = lax.axis_index("seq")
    shard_rows = cache_k.shape[0]
    page_slots = shard_rows // PAGE
    capacity = max(2, 2 * page_slots // shards)
    before = jnp.cumsum(page_counts) - page_counts
    my_pages = lax.dynamic_index_in_dim(page_counts, myself, keepdims=False)
    my_start = lax.dynamic_index_in_dim(before, myself, keepdims=False)
    local_row = jnp.arange(shard_rows, dtype=jnp.int32)
    usable = local_row < PAGE * my_pages
    places = PAGE * my_start + local_row
    prompt = PAGE * jnp.sum(page_counts)
    queries = lax.all_gather(prefill_q, "seq", axis=0, tiled=True)
    block_rows = queries.shape[0]
    query_places = prompt - block_rows + jnp.arange(block_rows, dtype=jnp.int32)
    allowed = usable[None, :] & (places[None, :] <= query_places[:, None])
    prefill_parts = partial_attend(queries, cache_k, cache_v, allowed)
    owners = page_owner[:, 0]
    page_index = jnp.arange(page_slots, dtype=jnp.int32)
    page_live = page_index < my_pages
    chosen = owners[:, None] == jnp.arange(shards, dtype=jnp.int32)[None, :]
    chosen_live = (chosen & page_live[:, None]).astype(jnp.int32)
    earlier = jnp.cumsum(chosen_live, axis=0) - chosen_live
    ranking = jnp.sum(earlier * chosen.astype(jnp.int32), axis=1)
    target = jnp.where(page_live, owners * capacity + ranking, shards * capacity)
    source_page = jnp.zeros((shards * capacity,), jnp.int32).at[target].set(page_index, mode="drop")
    filled = jnp.zeros((shards * capacity,), jnp.int32).at[target].set(1, mode="drop") > 0
    outgoing_k = jnp.where(filled[:, None], cache_k.reshape(page_slots, PAGE * KVD)[source_page], 0)
    outgoing_v = jnp.where(filled[:, None], cache_v.reshape(page_slots, PAGE * KVD)[source_page], 0)
    outgoing_ids = jnp.where(filled, myself * page_slots + source_page, -1)
    incoming_k, incoming_v, store_page = (
        lax.all_to_all(outgoing_k, "seq", split_axis=0, concat_axis=0, tiled=True),
        lax.all_to_all(outgoing_v, "seq", split_axis=0, concat_axis=0, tiled=True),
        lax.all_to_all(outgoing_ids, "seq", split_axis=0, concat_axis=0, tiled=True),
    )
    store_k = incoming_k.reshape(-1, KVD)
    store_v = incoming_v.reshape(-1, KVD)
    gathered_q, lengths = (
        lax.all_gather(decode_q, "seq", axis=0, tiled=True),
        lax.all_gather(context_len, "seq", axis=0, tiled=True),
    )
    requests = gathered_q.shape[0]
    query_rows = gathered_q.reshape(requests * STEPS, HQ * HD)
    limits = jnp.repeat(lengths, STEPS)
    page_device = store_page // page_slots
    page_within = store_page % page_slots
    device_hit = (page_device[:, None] == jnp.arange(shards, dtype=jnp.int32)[None, :]).astype(
        jnp.int32
    )
    page_begin = PAGE * (jnp.sum(device_hit * before[None, :], axis=1) + page_within)
    key_places = (page_begin[:, None] + jnp.arange(PAGE, dtype=jnp.int32)[None, :]).reshape(-1)
    key_usable = jnp.repeat(store_page >= 0, PAGE)
    decode_allowed = key_usable[None, :] & (key_places[None, :] < limits[:, None])
    decode_parts = partial_attend(query_rows, store_k, store_v, decode_allowed)

    def by_source(array):
        return array.reshape(shards, array.shape[0] // shards, array.shape[1])

    split_at = block_rows // shards
    joined_sums = jnp.concatenate((by_source(prefill_parts[0]), by_source(decode_parts[0])), axis=1)
    joined_highs = jnp.concatenate(
        (by_source(prefill_parts[1]), by_source(decode_parts[1])), axis=1
    )
    joined_totals = jnp.concatenate(
        (by_source(prefill_parts[2]), by_source(decode_parts[2])), axis=1
    )
    merged = combine_parts(
        (
            lax.all_to_all(joined_sums, "seq", split_axis=0, concat_axis=0, tiled=True),
            lax.all_to_all(joined_highs, "seq", split_axis=0, concat_axis=0, tiled=True),
            lax.all_to_all(joined_totals, "seq", split_axis=0, concat_axis=0, tiled=True),
        )
    )
    prefill_merged = (merged[0][:split_at], merged[1][:split_at], merged[2][:split_at])
    decode_merged = (merged[0][split_at:], merged[1][split_at:], merged[2][split_at:])
    prefill_sums, prefill_high, prefill_totals = prefill_merged
    own_rows = prefill_sums.shape[0]
    prefill_out = (
        (prefill_sums.reshape(own_rows, HQ, HD) / prefill_totals[:, :, None])
        .reshape(own_rows, HQ * HD)
        .astype(jnp.bfloat16)
    )
    weighted, highest, totals = decode_merged
    my_requests = decode_q.shape[0]
    grouping = HQ // KVH
    scaling = HD ** (-0.5)
    own_queries = decode_q.reshape(my_requests, STEPS, KVH, grouping, HD)
    own_keys = decode_k.reshape(my_requests, STEPS, KVH, HD)
    own_values = decode_v.reshape(my_requests, STEPS, KVH, HD)
    own_scores = (
        jnp.einsum("rsghd,rtgd->rsght", own_queries, own_keys, preferred_element_type=jnp.float32)
        * scaling
    )
    causal = jnp.arange(STEPS)[:, None] >= jnp.arange(STEPS)[None, :]
    own_scores = jnp.where(causal[None, :, None, None, :], own_scores, MASKED)
    own_high = jnp.max(own_scores, axis=4).reshape(my_requests * STEPS, HQ)
    overall = jnp.maximum(highest, own_high)
    factor = jnp.exp(highest - overall)
    own_weights = jnp.where(
        causal[None, :, None, None, :],
        jnp.exp(own_scores - overall.reshape(my_requests, STEPS, KVH, grouping)[..., None]),
        0.0,
    )
    totals = totals * factor + jnp.sum(own_weights, axis=4).reshape(my_requests * STEPS, HQ)
    own_product = jnp.einsum(
        "rsght,rtgd->rsghd",
        own_weights.astype(jnp.bfloat16),
        own_values,
        preferred_element_type=jnp.float32,
    )
    weighted = weighted.reshape(my_requests * STEPS, HQ, HD) * factor[
        :, :, None
    ] + own_product.reshape(my_requests * STEPS, HQ, HD)
    decode_out = (
        (weighted / totals[:, :, None]).reshape(my_requests, STEPS, HQ * HD).astype(jnp.bfloat16)
    )
    return (prefill_out, decode_out, store_k, store_v, store_page)


def solution(mesh):
    in_specs = (
        P(("groups", "seq"), None),
        P(("groups", "seq"), None),
        P(("groups", "seq"), None),
        P("groups"),
        P(("groups", "seq"), None),
        P(("groups", "seq"), None, None),
        P(("groups", "seq"), None, None),
        P(("groups", "seq"), None, None),
        P(("groups", "seq")),
    )
    out_specs = (
        P(("groups", "seq"), None),
        P(("groups", "seq"), None, None),
        P(("groups", "seq"), None),
        P(("groups", "seq"), None),
        P(("groups", "seq")),
    )
    return jax.shard_map(
        per_device, mesh=mesh, in_specs=in_specs, out_specs=out_specs, check_vma=False
    )
```

profile of v0, /device:TPU:15, one launch (start us, length us, event | category | flops | bytes accessed | tf_op | source)
XLA Modules:
  0.0 291.6 jit_solution(3598061653722434236)
XLA Ops:
  0.7 1.3 dynamic_slice.67
  3.5 0.8 select_reduce_fusion
  4.3 1.3 fusion.50
  7.9 6.5 %all-to-all-start = ((s32[16,8,1]{1,2,0:T(1,128)}), s32[16,8,1]{1,2,0:T(1,128)S(1)}, u32[]{:S(2)}, u32[]{:S(2)}) async-start(s32[16,8,1]{1,2,0:T(1,128)} %bitcast.10), calls=%async_computation | async-start | bytes 16384 | tf_op jit(solution)/shard_map/all_to_all | solution.py:105
  14.5 1.6 reshape.348
  16.6 3.2 %gather_fusion = bf16[128,8192]{1,0:T(8,128)(2,1)} fusion(bf16[64,8192]{1,0:T(8,128)(2,1)S(1)} %reshape.348, s32[1024]{0:T(1024)S(1)} %pad_clamp_fusion), kind=kCustom, calls=%fused_computation | custom fusion | bytes 4194816 | tf_op jit(solution)/shard_map/gather | solution.py:99
  19.8 3.2 %gather_fusion.1 = bf16[128,8192]{1,0:T(8,128)(2,1)} fusion(bf16[64,8192]{1,0:T(8,128)(2,1)S(1)} %reshape.350, s32[1024]{0:T(1024)S(1)} %pad_clamp_fusion), kind=kCustom, calls=%fused_computation.1 | custom fusion | bytes 4194816 | tf_op jit(solution)/shard_map/gather | solution.py:100
  23.1 4.1 %bitcast_select_fusion = (bf16[16,8,8192]{2,1,0:T(8,128)(2,1)}, bf16[16,8,8192]{2,1,0:T(8,128)(2,1)}) fusion(bf16[128,8192]{1,0:T(8,128)(2,1)} %gather_fusion.1, pred[16,8]{1,0:T(8,128)(4,1)S(1)} %broadcast_in_dim.195, bf16[128,8192]{1,0:T(8,128)(2,1)S(1)} %copy-done.1), kind=kLoop, calls=%fused_computation.45 | loop fusion | flops 2097152 | bytes 8388736 | tf_op jit(solution)/shard_map/jit(_where)/select_n | solution.py:100
  27.2 6.2 %all-to-all-start.1 = ((bf16[16,8,8192]{2,1,0:T(8,128)(2,1)}), bf16[16,8,8192]{2,1,0:T(8,128)(2,1)S(1)}, u32[]{:S(2)}, u32[]{:S(2)}) async-start(bf16[16,8,8192]{2,1,0:T(8,128)(2,1)} %get-tuple-element.510), calls=%async_computation.1 | async-start | bytes 4194304 | tf_op jit(solution)/shard_map/all_to_all | solution.py:103
  36.8 55.6 %all-gather = bf16[16,1,8192]{2,1,0:T(2,128)(2,1)S(1)} all-gather(bf16[1,1,8192]{2,1,0:T(2,128)(2,1)S(1)} %bitcast.166), channel_id=1, replica_groups=mesh['groups'=2,'seq'=16] {'seq'}, dimensions={0}, use_global_device_ids=true | all-gather | bytes 278528 | tf_op jit(solution)/shard_map/all_gather | solution.py:84
  94.7 4.6 %all-to-all-start.2 = ((bf16[16,8,8192]{2,1,0:T(8,128)(2,1)}), bf16[16,8,8192]{2,1,0:T(8,128)(2,1)}, u32[]{:S(2)}, u32[]{:S(2)}) async-start(bf16[16,8,8192]{2,1,0:T(8,128)(2,1)} %get-tuple-element.509), calls=%async_computation.2 | async-start | bytes 4194304 | tf_op jit(solution)/shard_map/all_to_all | solution.py:104
  99.4 25.8 %while.40 = (s32[]{:T(128)}, f32[16,8192]{1,0:T(8,128)S(1)}, f32[16,64]{1,0:T(8,128)S(1)}, f32[16,64]{1,0:T(8,128)S(1)}, bf16[16,8192]{1,0:T(8,128)(2,1)S(1)}, /...) while((s32[]{:T(128)}, f32[16,8192]{1,0:T(8,128)S(1)}, ...), condition=%wide.region_5.6_spmd.clone, body=%wide.region_2.5_spmd.clone.sunk | while | flops 34160392 | bytes 1448831 | solution.py:55
  99.5 1.2 fusion.78
  100.7 1.1 fusion.79
  102.7 1.2 fusion.78
  103.9 1.1 fusion.79
  105.9 1.2 fusion.78
  107.1 1.1 fusion.79
  109.1 1.2 fusion.78
  110.3 1.1 fusion.79
  112.3 1.2 fusion.78
  113.5 1.1 fusion.79
  115.6 1.2 fusion.78
  116.8 1.1 fusion.79
  118.8 1.2 fusion.78
  120.0 1.1 fusion.79
  122.0 1.2 fusion.78
  123.2 1.1 fusion.79
  125.1 19.5 %all-reduce = s32[16]{0:T(128)S(1)} all-reduce(s32[16]{0:T(128)S(1)} %dynamic-update-slice), channel_id=1, replica_groups=mesh['groups'=2,'seq'=16] {'seq'}, use_global_device_ids=true, to_apply=%add | all-reduce | flops 16 | bytes 128
  144.8 20.3 %all_gather.11 = bf16[16,2,8192]{2,1,0:T(2,128)(2,1)S(1)} all-gather(bf16[1,2,8192]{2,1,0:T(2,128)(2,1)S(1)} %copy-done.5), channel_id=1, replica_groups=mesh['groups'=2,'seq'=16] {'seq'}, dimensions={0}, use_global_device_ids=true | all-gather | bytes 557056 | tf_op jit(solution)/shard_map/all_gather | solution.py:110
  165.1 1.0 reshape.347
  166.0 1.3 reshape.346
  169.2 2.3 reshape.349
  171.5 2.9 reshape.351
  174.4 1.1 broadcast_in_dim.189
  175.5 35.4 %while.41 = (s32[]{:T(128)}, f32[32,8192]{1,0:T(8,128)}, f32[32,64]{1,0:T(8,128)S(1)}, f32[32,64]{1,0:T(8,128)S(1)}, bf16[32,8192]{1,0:T(8,128)(2,1)}, /*index=5...) while((s32[]{:T(128)}, f32[32,8192]{1,0:T(8,128)}, ...), condition=%wide.region_14.15_spmd.clone, body=%wide.region_11.14_spmd.clone.sunk | while | flops 136642048 | bytes 4551103 | solution.py:55
  175.5 0.8 dynamic-slice_bitcast_fusion.5
  176.4 1.4 fusion.84
  179.7 0.9 dynamic-slice_bitcast_fusion.5
  180.7 1.4 fusion.84
  184.1 0.9 dynamic-slice_bitcast_fusion.5
  185.1 1.4 fusion.84
  188.6 0.9 dynamic-slice_bitcast_fusion.5
  189.6 1.4 fusion.84
  193.0 0.9 dynamic-slice_bitcast_fusion.5
  194.0 1.4 fusion.84
  197.5 0.9 dynamic-slice_bitcast_fusion.5
  198.5 1.4 fusion.84
  202.0 0.9 dynamic-slice_bitcast_fusion.5
  202.9 1.4 fusion.84
  206.4 0.9 dynamic-slice_bitcast_fusion.5
  207.4 1.4 fusion.84
  210.9 0.9 reshape.429
  211.8 7.9 %all-to-all-start.4 = ((f32[16,1,192]{2,1,0:T(1,128)}), f32[16,1,192]{2,1,0:T(1,128)S(1)}, u32[]{:S(2)}, u32[]{:S(2)}) async-start(f32[16,1,192]{2,1,0:T(1,128)} %reshape.429), calls=%async_computation.4 | async-start | bytes 32768 | tf_op jit(solution)/shard_map/all_to_all | solution.py:141
  220.4 1.8 reshape.352
  222.3 1.6 all-to-all-done.4
  223.9 5.8 %all-to-all-start.5 = ((f32[16,1,192]{2,1,0:T(1,128)}), f32[16,1,192]{2,1,0:T(1,128)S(1)}, u32[]{:S(2)}, u32[]{:S(2)}) async-start(f32[16,1,192]{2,1,0:T(1,128)} %reshape.431), calls=%async_computation.5 | async-start | bytes 32768 | tf_op jit(solution)/shard_map/all_to_all | solution.py:142
  229.7 3.3 %pad_maximum_fusion = f32[16,3,8192]{2,1,0:T(4,128)} fusion(f32[16,2,8192]{2,1,0:T(2,128)S(1)} %reshape.352, f32[16,1,8192]{2,1,0:T(1,128)} %reshape.346), kind=kLoop, calls=%fused_computation.44 | loop fusion | flops 393216 | bytes 3145728 | tf_op jit(solution)/shard_map/concatenate | solution.py:131
  233.0 0.8 all-to-all-done.5
  233.8 6.0 %all-to-all-start.3 = ((f32[16,3,8192]{2,1,0:T(4,128)}), f32[16,3,8192]{2,1,0:T(4,128)S(1)}, u32[]{:S(2)}, u32[]{:S(2)}) async-start(f32[16,3,8192]{2,1,0:T(4,128)} %pad_maximum_fusion), calls=%async_computation.3 | async-start | bytes 4194304 | tf_op jit(solution)/shard_map/all_to_all | solution.py:140
  242.7 1.7 mul.187
  244.3 2.6 mul.188
  247.3 40.0 %all-to-all-done.3 = f32[16,3,8192]{2,1,0:T(4,128)S(1)} async-done(((f32[16,3,8192]{2,1,0:T(4,128)}), f32[16,3,8192]{2,1,0:T(4,128)S(1)}, u32[]{:S(2)}, u32[]{:S(2)}) %all-to-all-start.3) | async-done | bytes 1572896 | tf_op jit(solution)/shard_map/all_to_all | solution.py:140
  287.3 2.9 fusion.34
  (208 shorter events, 38.5 us)
Async XLA Ops:
  0.6 246.3 %copy-start = (bf16[1,2,1024]{2,1,0:T(2,128)(2,1)S(1)}, bf16[1,2,1024]{2,1,0:T(2,128)(2,1)}, u32[]{:S(2)}) copy-start(bf16[1,2,1024]{2,1,0:T(2,128)(2,1)} %param.20) | copy-start | bytes 12292
  0.6 15.4 %copy-start.3 = (bf16[512,1024]{1,0:T(8,128)(2,1)S(1)}, bf16[512,1024]{1,0:T(8,128)(2,1)}, u32[]{:S(2)}) copy-start(bf16[512,1024]{1,0:T(8,128)(2,1)} %param.15) | copy-start | bytes 3145732
  7.9 19.3 %all-to-all-start = ((s32[16,8,1]{1,2,0:T(1,128)}), s32[16,8,1]{1,2,0:T(1,128)S(1)}, u32[]{:S(2)}, u32[]{:S(2)}) async-start(s32[16,8,1]{1,2,0:T(1,128)} %bitcast.10), calls=%async_computation | async-start | bytes 16384 | tf_op jit(solution)/shard_map/all_to_all | solution.py:105
  19.8 3.3 %copy-start.1 = (bf16[128,8192]{1,0:T(8,128)(2,1)S(1)}, bf16[128,8192]{1,0:T(8,128)(2,1)}, u32[]{:S(2)}) copy-start(bf16[128,8192]{1,0:T(8,128)(2,1)} %gather_fusion) | copy-start | bytes 6291460
  27.2 6.2 %copy-start.6 = (s32[16]{0:T(128)S(1)}, s32[16]{0:T(128)}, u32[]{:S(2)}) copy-start(s32[16]{0:T(128)} %param.16) | copy-start | bytes 196
  27.2 9.6 %copy-start.4 = (bf16[1,8192]{1,0:T(2,128)(2,1)S(1)}, bf16[1,8192]{1,0:T(2,128)(2,1)}, u32[]{:S(2)}) copy-start(bf16[1,8192]{1,0:T(2,128)(2,1)} %param.13) | copy-start | bytes 49156
  27.2 65.5 %copy-start.9 = (u32[32]{0:T(128)S(1)}, u32[32]{0:T(128)}, u32[]{:S(2)}) copy-start(u32[32]{0:T(128)} %constant.304) | copy-start | bytes 388
  27.2 67.5 %all-to-all-start.1 = ((bf16[16,8,8192]{2,1,0:T(8,128)(2,1)}), bf16[16,8,8192]{2,1,0:T(8,128)(2,1)S(1)}, u32[]{:S(2)}, u32[]{:S(2)}) async-start(bf16[16,8,8192]{2,1,0:T(8,128)(2,1)} %get-tuple-element.510), calls=%async_computation.1 | async-start | bytes 4194304 | tf_op jit(solution)/shard_map/all_to_all | solution.py:103
  94.7 76.8 %all-to-all-start.2 = ((bf16[16,8,8192]{2,1,0:T(8,128)(2,1)}), bf16[16,8,8192]{2,1,0:T(8,128)(2,1)}, u32[]{:S(2)}, u32[]{:S(2)}) async-start(bf16[16,8,8192]{2,1,0:T(8,128)(2,1)} %get-tuple-element.509), calls=%async_computation.2 | async-start | bytes 4194304 | tf_op jit(solution)/shard_map/all_to_all | solution.py:104
  99.3 45.4 %copy-start.5 = (bf16[1,2,8192]{2,1,0:T(2,128)(2,1)S(1)}, bf16[1,2,8192]{2,1,0:T(2,128)(2,1)}, u32[]{:S(2)}) copy-start(bf16[1,2,8192]{2,1,0:T(2,128)(2,1)} %param.18) | copy-start | bytes 98308
  168.6 2.9 copy-start.7
  210.8 22.2 %copy-start.2 = (bf16[1024,1024]{1,0:T(8,128)(2,1)}, bf16[1024,1024]{1,0:T(8,128)(2,1)S(1)}, u32[]{:S(2)}) copy-start(bf16[1024,1024]{1,0:T(8,128)(2,1)S(1)} %get-tuple-element.754) | copy-start | bytes 6291460
  211.8 12.1 %all-to-all-start.4 = ((f32[16,1,192]{2,1,0:T(1,128)}), f32[16,1,192]{2,1,0:T(1,128)S(1)}, u32[]{:S(2)}, u32[]{:S(2)}) async-start(f32[16,1,192]{2,1,0:T(1,128)} %reshape.429), calls=%async_computation.4 | async-start | bytes 32768 | tf_op jit(solution)/shard_map/all_to_all | solution.py:141
  223.9 10.0 %all-to-all-start.5 = ((f32[16,1,192]{2,1,0:T(1,128)}), f32[16,1,192]{2,1,0:T(1,128)S(1)}, u32[]{:S(2)}, u32[]{:S(2)}) async-start(f32[16,1,192]{2,1,0:T(1,128)} %reshape.431), calls=%async_computation.5 | async-start | bytes 32768 | tf_op jit(solution)/shard_map/all_to_all | solution.py:142
  233.0 6.8 %copy-start.8 = (bf16[1,2,1024]{2,1,0:T(2,128)(2,1)S(1)}, bf16[1,2,1024]{2,1,0:T(2,128)(2,1)}, u32[]{:S(2)}) copy-start(bf16[1,2,1024]{2,1,0:T(2,128)(2,1)} %param.19) | copy-start | bytes 12292
  233.8 53.4 %all-to-all-start.3 = ((f32[16,3,8192]{2,1,0:T(4,128)}), f32[16,3,8192]{2,1,0:T(4,128)S(1)}, u32[]{:S(2)}, u32[]{:S(2)}) async-start(f32[16,3,8192]{2,1,0:T(4,128)} %pad_maximum_fusion), calls=%async_computation.3 | async-start | bytes 4194304 | tf_op jit(solution)/shard_map/all_to_all | solution.py:140
where the time goes:
time: 293 us; the launch traced here: 292 us
  blocking collectives  95.3 us (33%)
  local copies, waits for them, and re-layouts  54 us (18%)
  waiting for transfers between devices  42.4 us (14%)
  starting transfers between devices  37 us (13%)
  matrix products  33.4 us (11%)
  other arithmetic  24.9 us (8%)
  between operations  3.66 us (1%)
    all_gather x1, blocking collectives, per_device(): queries = lax.all_gather(prefill_q, 'seq', axis=0, tiled=True)  55.6 us
    all_to_all x1, waiting for transfers between devices, per_device(): lax.all_to_all(joined_sums, 'seq', split_axis=0, concat_axis=0, tiled=True)  40 us
    dot_general x16, matrix products, one_group(): jnp.einsum('qhd,kd->qhk', query_group, key_group, preferred_element_type=...  20.6 us
    all_gather x1, blocking collectives, per_device(): lax.all_gather(decode_q, 'seq', axis=0, tiled=True)  20.3 us
    unnamed x1, blocking collectives  19.5 us
    dot_general x16, matrix products, one_group(): jnp.einsum('qhk,kd->qhd', weights.astype(jnp.bfloat16), value_group, pref...  12.3 us
    all_to_all x1, starting transfers between devices, per_device(): lax.all_to_all(joined_highs, 'seq', split_axis=0, concat_axis=0, tiled=True)  7.89 us
    while x32, local copies, waits for them, and re-layouts  7 us
  transfers between devices with their start and end apart: 6, of which 3 were waited for; matrix products, arithmetic and copies ran while one was open for 21% of the time, Pallas kernels for 0%

commit v1 on v0

v1 whole, which is shorter than its diff:
```python
import functools

import jax
import jax.numpy as jnp
from jax import lax
from jax.experimental import pallas as pl
from jax.experimental.pallas import tpu as pltpu
from jax.sharding import PartitionSpec as P

HQ = 64
KVH = 8
HD = 128
PAGE = 8
STEPS = 2
KVD = 1024
GROUP = HQ // KVH
ROWS = (1 + STEPS) * GROUP
LANES = 128
ID_LANE = 64
MASKED = -1e30
SCALE = HD ** (-0.5)
MESH = pl.DeviceIdType.MESH

Q, META, KEYS, VALUES, PART, STAT = range(6)


def pack_kernel(n, cap, page_slots, owner, counts, context, ck, cv, out_k, out_v, meta, table, seen):
    dst = pl.program_id(0)
    me = lax.axis_index("seq")

    @pl.when(dst == 0)
    def _():
        def clear(i, _):
            table[i] = -1
            return 0

        lax.fori_loop(0, n * cap, clear, 0)

        def clear_seen(i, _):
            seen[i] = 0
            return 0

        lax.fori_loop(0, n, clear_seen, 0)

        def place(j, _):
            o = owner[j]
            k = seen[o]
            seen[o] = k + 1
            table[o * cap + k] = j
            return 0

        lax.fori_loop(0, counts[me], place, 0)

    tile_row = lax.broadcasted_iota(jnp.int32, (8, LANES), 0)
    ids = jnp.full((8, LANES), -1, jnp.int32)
    for k in range(cap):
        src = table[dst * cap + k]
        ids = jnp.where(tile_row == k, jnp.where(src >= 0, me * page_slots + src, -1), ids)

        @pl.when(src >= 0)
        def _():
            out_k[k] = ck[src]
            out_v[k] = cv[src]

        @pl.when(src < 0)
        def _():
            out_k[k] = jnp.zeros((PAGE, KVD), out_k.dtype)
            out_v[k] = jnp.zeros((PAGE, KVD), out_v.dtype)

    lane = lax.broadcasted_iota(jnp.int32, (8, LANES), 1)
    meta[0] = jnp.where(lane < ID_LANE, context[0], ids)


def pack(n, cap, owner, counts, context, ck, cv):
    page_slots = ck.shape[0]
    smem = pl.BlockSpec(memory_space=pltpu.SMEM)
    whole = pl.BlockSpec(ck.shape, lambda d: (0, 0, 0))
    block = pl.BlockSpec((cap, PAGE, KVD), lambda d: (d, 0, 0))
    return pl.pallas_call(
        functools.partial(pack_kernel, n, cap, page_slots),
        grid=(n,),
        in_specs=[smem, smem, smem, whole, whole],
        out_specs=(block, block, pl.BlockSpec((1, 8, LANES), lambda d: (d, 0, 0))),
        out_shape=(
            jax.ShapeDtypeStruct((n * cap, PAGE, KVD), ck.dtype),
            jax.ShapeDtypeStruct((n * cap, PAGE, KVD), cv.dtype),
            jax.ShapeDtypeStruct((n, 8, LANES), jnp.int32),
        ),
        scratch_shapes=[pltpu.SMEM((n * cap,), jnp.int32), pltpu.SMEM((n,), jnp.int32)],
        name="pack",
    )(owner, counts, context, ck, cv)


def main_kernel(
    n, cap, chunk, bounds, q_ref, meta_ref, ck_ref, cv_ref, pk_ref, pv_ref, ok_ref, ov_ref,
    out_ref, store_k, store_v, meta_out,
    qbuf, obuf, stat, limit, pbuf, sbuf, send, recv, local,
):
    me = lax.axis_index("seq")

    def rows_of(d):
        return pl.ds(pl.multiple_of(d * ROWS, 8), ROWS)

    def slots_of(d):
        return pl.ds(d * cap, cap)

    def ends(kind, peer, writer):
        if kind == Q:
            return q_ref, qbuf.at[:, rows_of(writer), :]
        if kind == META:
            return meta_ref.at[peer], meta_out.at[writer]
        if kind == KEYS:
            return pk_ref.at[slots_of(peer)], store_k.at[slots_of(writer)]
        if kind == VALUES:
            return pv_ref.at[slots_of(peer)], store_v.at[slots_of(writer)]
        if kind == PART:
            return obuf.at[:, rows_of(peer), :], pbuf.at[writer]
        return stat.at[rows_of(peer), :], sbuf.at[writer]

    def outgoing(kind, peer):
        src, dst = ends(kind, peer, me)
        return pltpu.make_async_remote_copy(
            src_ref=src, dst_ref=dst, send_sem=send.at[kind, peer], recv_sem=recv.at[kind, me],
            device_id={"seq": peer}, device_id_type=MESH,
        )

    def incoming(kind, peer):
        src, dst = ends(kind, peer, peer)
        return pltpu.make_async_remote_copy(
            src_ref=src, dst_ref=dst, send_sem=send.at[kind, peer], recv_sem=recv.at[kind, peer],
            device_id={"seq": peer}, device_id_type=MESH,
        )

    def own(kind):
        src, dst = ends(kind, me, me)
        return pltpu.make_async_copy(src, dst, local.at[kind])

    def each_peer(body):
        def step(i, _):
            body(lax.rem(me + i, n))
            return 0

        lax.fori_loop(1, n, step, 0)

    barrier = pltpu.get_barrier_semaphore()
    each_peer(
        lambda peer: pl.semaphore_signal(
            barrier, inc=1, device_id={"seq": peer}, device_id_type=MESH
        )
    )
    pl.semaphore_wait(barrier, n - 1)

    def start_small(peer):
        outgoing(META, peer).start()
        outgoing(Q, peer).start()

    def start_pages(peer):
        outgoing(KEYS, peer).start()
        outgoing(VALUES, peer).start()

    each_peer(start_small)
    for kind in (META, Q, KEYS, VALUES):
        own(kind).start()
    each_peer(start_pages)

    own(META).wait()
    own(Q).wait()

    def wait_small(peer):
        incoming(META, peer).wait_recv()
        incoming(Q, peer).wait_recv()

    each_peer(wait_small)

    live, start, first = bounds[0], bounds[1], bounds[2]

    def set_limit(d, _):
        base = pl.multiple_of(d * ROWS, 8)
        context = jnp.broadcast_to(meta_out[d][:, 0:1], (8, LANES))
        reach = jnp.minimum(live, context - start)
        limit[pl.ds(base, 8), :] = jnp.full((8, LANES), jnp.minimum(live, first + d + 1 - start))
        for s in range(STEPS):
            limit[pl.ds(pl.multiple_of(base + 8 * (s + 1), 8), 8), :] = reach
        return 0

    lax.fori_loop(0, n, set_limit, 0)

    lane = lax.broadcasted_iota(jnp.int32, (chunk, LANES), 1)
    keys = ck_ref.shape[0]

    def attend(c, _):
        rows = pl.ds(pl.multiple_of(c * chunk, 16), chunk)

        def head(g, stats):
            cols = pl.ds(pl.multiple_of(g * HD, HD), HD)
            scores = lax.dot_general(
                qbuf[g, rows, :], ck_ref[:, cols], (((1,), (1,)), ((), ())),
                preferred_element_type=jnp.float32,
            ) * SCALE
            place = lax.broadcasted_iota(jnp.int32, (chunk, keys), 1)
            bound = limit[rows, 0:1]
            scores = jnp.where(place < bound, scores, MASKED)
            high = jnp.max(scores, axis=1, keepdims=True)
            weights = jnp.exp(scores - high)
            total = jnp.sum(weights, axis=1, keepdims=True)
            summed = jnp.dot(
                weights.astype(jnp.bfloat16), cv_ref[:, cols], preferred_element_type=jnp.float32
            )
            obuf[g, rows, :] = (summed / total).astype(jnp.bfloat16)
            level = jnp.where(bound > 0, high + jnp.log(total), MASKED)
            return jnp.where(lane == g, level, stats)

        stat[rows, :] = lax.fori_loop(0, KVH, head, jnp.zeros((chunk, LANES), jnp.float32))
        return 0

    lax.fori_loop(0, stat.shape[0] // chunk, attend, 0)

    def start_parts(peer):
        outgoing(STAT, peer).start()
        outgoing(PART, peer).start()

    each_peer(start_parts)
    own(STAT).start()
    own(PART).start()

    own_lane = lax.broadcasted_iota(jnp.int32, (ROWS, LANES), 1)
    own_row = lax.broadcasted_iota(jnp.int32, (ROWS, LANES), 0)
    own_levels = []
    for t in range(STEPS):
        level = jnp.zeros((ROWS, LANES), jnp.float32)
        for g in range(KVH):
            key = ok_ref[t : t + 1, g * HD : (g + 1) * HD].astype(jnp.float32)
            score = jnp.sum(q_ref[g].astype(jnp.float32) * key, axis=1, keepdims=True) * SCALE
            level = jnp.where(own_lane == g, score, level)
        own_levels.append(jnp.where(own_row >= GROUP * (t + 1), level, MASKED))

    own(STAT).wait()
    own(PART).wait()

    def wait_parts(peer):
        incoming(STAT, peer).wait_recv()
        incoming(PART, peer).wait_recv()

    each_peer(wait_parts)

    top = functools.reduce(jnp.maximum, own_levels)
    top = lax.fori_loop(0, n, lambda d, high: jnp.maximum(high, sbuf[d]), top)

    norm = jnp.zeros((ROWS, LANES), jnp.float32)
    sums = [jnp.zeros((ROWS, HD), jnp.float32) for _ in range(KVH)]
    for t in range(STEPS):
        factor = jnp.exp(own_levels[t] - top)
        norm = norm + factor
        for g in range(KVH):
            value = ov_ref[t : t + 1, g * HD : (g + 1) * HD].astype(jnp.float32)
            sums[g] = sums[g] + factor[:, g : g + 1] * value

    def add(d, state):
        norm, sums = state
        factor = jnp.exp(sbuf[d] - top)
        sums = tuple(
            sums[g] + factor[:, g : g + 1] * pbuf[d, g].astype(jnp.float32) for g in range(KVH)
        )
        return norm + factor, sums

    norm, sums = lax.fori_loop(0, n, add, (norm, tuple(sums)))
    for g in range(KVH):
        out_ref[g] = (sums[g] / norm[:, g : g + 1]).astype(out_ref.dtype)

    own(KEYS).wait()
    own(VALUES).wait()

    def finish(peer):
        incoming(KEYS, peer).wait_recv()
        incoming(VALUES, peer).wait_recv()
        for kind in (Q, META, KEYS, VALUES, PART, STAT):
            outgoing(kind, peer).wait_send()

    each_peer(finish)


def main(n, cap, bounds, q, meta, ck, cv, pk, pv, own_k, own_v):
    height = n * ROWS
    chunk = min(height, 384)
    vmem = pl.BlockSpec(memory_space=pltpu.VMEM)
    smem = pl.BlockSpec(memory_space=pltpu.SMEM)
    hbm = pl.BlockSpec(memory_space=pl.ANY)
    return pl.pallas_call(
        functools.partial(main_kernel, n, cap, chunk),
        in_specs=[smem, vmem, vmem, vmem, vmem, hbm, hbm, vmem, vmem],
        out_specs=(vmem, hbm, hbm, vmem),
        out_shape=(
            jax.ShapeDtypeStruct((KVH, ROWS, HD), jnp.bfloat16),
            jax.ShapeDtypeStruct(pk.shape, pk.dtype),
            jax.ShapeDtypeStruct(pv.shape, pv.dtype),
            jax.ShapeDtypeStruct(meta.shape, meta.dtype),
        ),
        scratch_shapes=[
            pltpu.VMEM((KVH, height, HD), jnp.bfloat16),
            pltpu.VMEM((KVH, height, HD), jnp.bfloat16),
            pltpu.VMEM((height, LANES), jnp.float32),
            pltpu.VMEM((height, LANES), jnp.int32),
            pltpu.VMEM((n, KVH, ROWS, HD), jnp.bfloat16),
            pltpu.VMEM((n, ROWS, LANES), jnp.float32),
            pltpu.SemaphoreType.DMA((6, n)),
            pltpu.SemaphoreType.DMA((6, n)),
            pltpu.SemaphoreType.DMA((6,)),
        ],
        compiler_params=pltpu.CompilerParams(
            collective_id=0, has_side_effects=True, vmem_limit_bytes=48 << 20
        ),
        name="exchange",
    )(bounds, q, meta, ck, cv, pk, pv, own_k, own_v)


def per_device(
    prefill_q, cache_k, cache_v, page_counts, page_owner, decode_q, decode_k, decode_v, context_len
):
    n = lax.axis_size("seq")
    me = lax.axis_index("seq")
    page_slots = cache_k.shape[0] // PAGE
    cap = max(2, 2 * page_slots // n)
    ck = cache_k.reshape(page_slots, PAGE, KVD)
    cv = cache_v.reshape(page_slots, PAGE, KVD)
    pk, pv, meta = pack(n, cap, page_owner[:, 0], page_counts, context_len, ck, cv)
    position = jnp.arange(n, dtype=jnp.int32)
    bounds = PAGE * jnp.stack(
        [
            jnp.sum(jnp.where(position == me, page_counts, 0)),
            jnp.sum(jnp.where(position < me, page_counts, 0)),
            jnp.sum(page_counts),
        ]
    ) - jnp.array([0, 0, n], jnp.int32)
    q = jnp.concatenate((prefill_q, decode_q[0]), axis=0)
    q = q.reshape(1 + STEPS, KVH, GROUP, HD).transpose(1, 0, 2, 3).reshape(KVH, ROWS, HD)
    out, store_k, store_v, meta = main(
        n, cap, bounds, q, meta, cache_k, cache_v, pk, pv, decode_k[0], decode_v[0]
    )
    out = out.reshape(KVH, 1 + STEPS, GROUP, HD).transpose(1, 0, 2, 3).reshape(1 + STEPS, HQ * HD)
    return (
        out[:1],
        out[1:].reshape(1, STEPS, HQ * HD),
        store_k.reshape(-1, KVD),
        store_v.reshape(-1, KVD),
        meta[:, :cap, ID_LANE].reshape(-1),
    )


def solution(mesh):
    both = ("groups", "seq")
    in_specs = (
        P(both, None),
        P(both, None),
        P(both, None),
        P("groups"),
        P(both, None),
        P(both, None, None),
        P(both, None, None),
        P(both, None, None),
        P(both),
    )
    out_specs = (
        P(both, None),
        P(both, None, None),
        P(both, None),
        P(both, None),
        P(both),
    )
    return jax.shard_map(
        per_device, mesh=mesh, in_specs=in_specs, out_specs=out_specs, check_vma=False
    )
```

time: 293 us -> 166 us (0.57)
  Pallas kernels: 0 us -> 149 us
  blocking collectives: 95.3 us -> 0 us
  local copies, waits for them, and re-layouts: 54 us -> 9.01 us
  waiting for transfers between devices: 42.4 us -> 0 us
  starting transfers between devices: 37 us -> 0 us
  matrix products: 33.4 us -> 0 us
  other arithmetic: 24.9 us -> 5.62 us
    pallas_call x0 -> x2, Pallas kernels: none -> 149 us  [the longest x1 140 us: main(): pl.pallas_call(functools.partial(main_kernel, n, cap, chunk), in_specs=[s...]
    all_gather x2 -> x0, blocking collectives: 75.8 us -> none  [the longest x1 55.6 us: per_device(): queries = lax.all_gather(prefill_q, 'seq', axis=0, tiled=True)]
    all_to_all x6 -> x0, waiting for transfers between devices: 42.4 us -> none  [the longest x1 40 us: per_device(): lax.all_to_all(joined_sums, 'seq', split_axis=0, concat_axis=0, tiled=True)]
    all_to_all x6 -> x0, starting transfers between devices: 37 us -> none  [the longest x1 7.89 us: per_device(): lax.all_to_all(joined_highs, 'seq', split_axis=0, concat_axis=0, tiled=True)]
    dot_general x34 -> x0, matrix products: 33.4 us -> none  [the longest x16 20.6 us: one_group(): jnp.einsum('qhd,kd->qhk', query_group, key_group, preferred_element_type=...]
    unnamed x1 -> x0, blocking collectives: 19.5 us -> none
    dynamic_update_slice x48 -> x0, local copies, waits for them, and re-layouts: 14.1 us -> none  [the longest x16 5.6 us: one_group(): lax.dynamic_update_slice_in_dim(weighted, product.reshape(height, groupin...]
    reshape x10 -> x1, local copies, waits for them, and re-layouts: 11.7 us -> 0.63 us  [per_device(): out[1:].reshape(1, STEPS, HQ * HD)]
  transfers between devices with their start and end apart: 6 -> 0, of which waited for: 3 -> 0; matrix products, arithmetic and copies ran while one was open for 21% -> 0% of each run, Pallas kernels for 0% -> 0%
where the time goes in v1:
time: 166 us; the launch traced here: 165 us
  Pallas kernels  149 us (90%)
  local copies, waits for them, and re-layouts  9.01 us (5%)
  other arithmetic  5.62 us (3%)
    pallas_call x1, Pallas kernels, main(): pl.pallas_call(functools.partial(main_kernel, n, cap, chunk), in_specs=[s...  140 us
    pallas_call x1, Pallas kernels, pack(): pl.pallas_call(functools.partial(pack_kernel, n, cap, page_slots), grid=(...  9.41 us
    unnamed x16, local copies, waits for them, and re-layouts  6.72 us

profile of v1, /device:TPU:15, one launch (start us, length us, event | category | flops | bytes accessed | tf_op | source)
XLA Modules:
  0.0 165.4 jit_solution(3609333810724720472)
XLA Ops:
  0.6 0.0 copy-start.1
  0.6 0.0 copy-start
  0.7 0.0 copy-start.5
  0.7 0.0 copy-start.4
  1.5 1.3 fusion
  2.8 2.7 %fusion.2.bounds = s32[3]{0:T(128)S(1)} fusion(s32[3]{0:T(128)} %constant.16, s32[1]{0:T(128)} %bitcast.2, s32[1]{0:T(128)} %bitcast.1, s32[1]{0:T(128)} %bitcast), kind=kLoop, calls=%fused_computation.8 | loop fusion | flops 12 | bytes 36 | tf_op jit(solution)/shard_map/sub | solution.py:327
  5.5 0.8 reduce
  6.3 0.8 maximum_bitcast_fusion.q_ref
  7.1 9.4 %pack.1 = (bf16[128,8,1024]{2,1,0:T(8,128)(2,1)}, bf16[128,8,1024]{2,1,0:T(8,128)(2,1)}, s32[16,8,128]{2,1,0:T(8,128)}) custom-call(s32[64]{0:T(128)} %bitcast.43, s32[16]{0:T(128)} %counts.1, s32[1]{0:T(128)S(6)} %copy.29.context, bf16[64,8,1024]{2,1,0:T(8,128)(2,1)} %bitcast.33, bf16[64,8,1024]{2,1,0:T(8,128)(2,1)} %bitcast.34), custom_call_target="tpu_custom_call" | custom-call | tf_op jit(solution)/shard_map/pack/pallas_call | solution.py:79
  16.5 0.0 copy-done.1
  16.5 0.0 copy-done
  16.5 0.0 copy-done.5
  16.5 0.0 copy-done.4
  16.5 0.0 copy-start.3
  16.6 0.8 copy-done.3
  17.4 139.9 %exchange.1 = (bf16[8,24,128]{2,1,0:T(8,128)(2,1)S(1)}, bf16[128,8,1024]{2,1,0:T(8,128)(2,1)S(1)}, bf16[128,8,1024]{2,1,0:T(8,128)(2,1)}, s32[16,8,128]{2,1,0:T(8,128)S(1)}) custom-call(s32[3]{0:T(128)S(1)} %fusion.2.bounds, bf16[8,24,128]{2,1,0:T(8,128)(2,1)S(1)} %maximum_bitcast_fusion.q_ref, s32[16,8,128]{2,1,0:T(8,128)S(1)} %copy-done.3, ...), custom_call_target="tpu_custom_call" | custom-call | tf_op jit(solution)/shard_map/exchange/pallas_call | solution.py:288
  157.3 0.0 copy-start.2
  157.3 1.3 copy-done.2
  158.6 0.4 slice_reduce_fusion
  159.0 0.6 reshape_squeeze.3
  159.6 0.6 reshape.43
  160.2 0.6 slice.14
  160.9 0.0 copy-start.6
  160.9 3.2 %copy.30 = bf16[1024,1024]{1,0:T(8,128)(2,1)} copy(bf16[1024,1024]{1,0:T(8,128)(2,1)} %bitcast.35) | data formatting | bytes 4194304
  164.1 0.0 copy-done.6
  164.1 1.3 copy.31
  (3 shorter events, 0.0 us)
Async XLA Ops:
  0.6 15.9 %copy-start.1 = (bf16[512,1024]{1,0:T(8,128)(2,1)S(1)}, bf16[512,1024]{1,0:T(8,128)(2,1)}, u32[]{:S(2)}) copy-start(bf16[512,1024]{1,0:T(8,128)(2,1)} %cv_ref.1) | copy-start | bytes 3145732
  0.6 15.9 %copy-start = (bf16[512,1024]{1,0:T(8,128)(2,1)S(1)}, bf16[512,1024]{1,0:T(8,128)(2,1)}, u32[]{:S(2)}) copy-start(bf16[512,1024]{1,0:T(8,128)(2,1)} %ck_ref.1) | copy-start | bytes 3145732
  0.7 15.9 %copy-start.5 = (bf16[1,2,1024]{2,1,0:T(2,128)(2,1)S(1)}, bf16[1,2,1024]{2,1,0:T(2,128)(2,1)}, u32[]{:S(2)}) copy-start(bf16[1,2,1024]{2,1,0:T(2,128)(2,1)} %param.17) | copy-start | bytes 12292
  0.7 15.9 %copy-start.4 = (bf16[1,2,1024]{2,1,0:T(2,128)(2,1)S(1)}, bf16[1,2,1024]{2,1,0:T(2,128)(2,1)}, u32[]{:S(2)}) copy-start(bf16[1,2,1024]{2,1,0:T(2,128)(2,1)} %param.16) | copy-start | bytes 12292
  16.5 0.8 copy-start.3
  157.3 1.3 copy-start.2
  160.9 3.2 %copy-start.6 = (bf16[128,8,1024]{2,1,0:T(8,128)(2,1)S(1)}, bf16[128,8,1024]{2,1,0:T(8,128)(2,1)}, u32[]{:S(2)}) copy-start(bf16[128,8,1024]{2,1,0:T(8,128)(2,1)} %get-tuple-element.17) | copy-start | bytes 6291460

commit v2 on v1

--- a/solution.py
+++ b/solution.py
@@ -21,7 +21,8 @@
 SCALE = HD ** (-0.5)
 MESH = pl.DeviceIdType.MESH
 
-Q, META, KEYS, VALUES, PART, STAT = range(6)
+META, KEYS, VALUES = range(3)
+QROW, PART, STAT = range(3)
 
 
 def pack_kernel(n, cap, page_slots, owner, counts, context, ck, cv, out_k, out_v, meta, table, seen):
@@ -92,98 +93,137 @@
 
 
 def main_kernel(
-    n, cap, chunk, bounds, q_ref, meta_ref, ck_ref, cv_ref, pk_ref, pv_ref, ok_ref, ov_ref,
+    n, cap, chunk, counts, q_ref, meta_ref, ck_ref, cv_ref, pk_ref, pv_ref, ok_ref, ov_ref,
     out_ref, store_k, store_v, meta_out,
-    qbuf, obuf, stat, limit, pbuf, sbuf, send, recv, local,
+    qbuf, obuf, stat, limit, got1, got1s, obuf1, stat1, got2, got2s, obuf2, stat2, pbuf, sbuf,
+    page_send, page_recv, row_send, row_recv, pair_send, pair_recv, local,
 ):
+    depth = n // 4
     me = lax.axis_index("seq")
-
-    def rows_of(d):
-        return pl.ds(pl.multiple_of(d * ROWS, 8), ROWS)
+    my_z, my_y, my_c = me // 4, (me // 2) % 2, me % 2
+    block = (my_c * 2 + my_y) * depth + my_z
+    across = my_z * 4 + (1 - my_y) * 2 + my_c
+    sibling = my_z * 4 + my_y * 2 + (1 - my_c)
+
+    def rows_of(first, count=1):
+        return pl.ds(pl.multiple_of(first * ROWS, 8), count * ROWS)
 
     def slots_of(d):
         return pl.ds(d * cap, cap)
 
-    def ends(kind, peer, writer):
-        if kind == Q:
-            return q_ref, qbuf.at[:, rows_of(writer), :]
+    def page_ends(kind, peer, writer):
         if kind == META:
             return meta_ref.at[peer], meta_out.at[writer]
         if kind == KEYS:
             return pk_ref.at[slots_of(peer)], store_k.at[slots_of(writer)]
-        if kind == VALUES:
-            return pv_ref.at[slots_of(peer)], store_v.at[slots_of(writer)]
-        if kind == PART:
-            return obuf.at[:, rows_of(peer), :], pbuf.at[writer]
-        return stat.at[rows_of(peer), :], sbuf.at[writer]
-
-    def outgoing(kind, peer):
-        src, dst = ends(kind, peer, me)
+        return pv_ref.at[slots_of(peer)], store_v.at[slots_of(writer)]
+
+    def page(kind, peer, arriving=False):
+        src, dst = page_ends(kind, peer, peer if arriving else me)
         return pltpu.make_async_remote_copy(
-            src_ref=src, dst_ref=dst, send_sem=send.at[kind, peer], recv_sem=recv.at[kind, me],
+            src_ref=src, dst_ref=dst, send_sem=page_send.at[kind, peer],
+            recv_sem=page_recv.at[kind, peer if arriving else me],
             device_id={"seq": peer}, device_id_type=MESH,
         )
 
-    def incoming(kind, peer):
-        src, dst = ends(kind, peer, peer)
+    def row_ends(kind, z, writer):
+        if kind == QROW:
+            return q_ref, qbuf.at[:, rows_of((my_c * 2 + my_y) * depth + writer), :]
+        if kind == PART:
+            return obuf2.at[:, rows_of(z), :], pbuf.at[writer]
+        return stat2.at[rows_of(z), :], sbuf.at[writer]
+
+    def row(kind, z, arriving=False):
+        src, dst = row_ends(kind, z, z if arriving else my_z)
         return pltpu.make_async_remote_copy(
-            src_ref=src, dst_ref=dst, send_sem=send.at[kind, peer], recv_sem=recv.at[kind, peer],
+            src_ref=src, dst_ref=dst, send_sem=row_send.at[kind, z],
+            recv_sem=row_recv.at[kind, z if arriving else my_z],
+            device_id={"seq": z * 4 + my_y * 2 + my_c}, device_id_type=MESH,
+        )
+
+    def pair(number, src, dst, peer):
+        return pltpu.make_async_remote_copy(
+            src_ref=src, dst_ref=dst, send_sem=pair_send.at[number], recv_sem=pair_recv.at[number],
             device_id={"seq": peer}, device_id_type=MESH,
         )
 
-    def own(kind):
-        src, dst = ends(kind, me, me)
+    def own_page(kind):
+        src, dst = page_ends(kind, me, me)
         return pltpu.make_async_copy(src, dst, local.at[kind])
 
-    def each_peer(body):
+    def own_row(kind):
+        src, dst = row_ends(kind, my_z, my_z)
+        return pltpu.make_async_copy(src, dst, local.at[3 + kind])
+
+    def each(count, mine, body):
         def step(i, _):
-            body(lax.rem(me + i, n))
+            body(lax.rem(mine + i, count))
             return 0
 
-        lax.fori_loop(1, n, step, 0)
+        lax.fori_loop(1, count, step, 0)
 
     barrier = pltpu.get_barrier_semaphore()
-    each_peer(
-        lambda peer: pl.semaphore_signal(
-            barrier, inc=1, device_id={"seq": peer}, device_id_type=MESH
-        )
-    )
+
+    def greet(peer):
+        pl.semaphore_signal(barrier, inc=1, device_id={"seq": peer}, device_id_type=MESH)
+
+    each(n, me, greet)
     pl.semaphore_wait(barrier, n - 1)
 
-    def start_small(peer):
-        outgoing(META, peer).start()
-        outgoing(Q, peer).start()
+    each(depth, my_z, lambda z: row(QROW, z).start())
+    own_row(QROW).start()
+    each(n, me, lambda peer: page(META, peer).start())
+    for kind in (META, KEYS, VALUES):
+        own_page(kind).start()
 
     def start_pages(peer):
-        outgoing(KEYS, peer).start()
-        outgoing(VALUES, peer).start()
-
-    each_peer(start_small)
-    for kind in (META, Q, KEYS, VALUES):
-        own(kind).start()
-    each_peer(start_pages)
-
-    own(META).wait()
-    own(Q).wait()
-
-    def wait_small(peer):
-        incoming(META, peer).wait_recv()
-        incoming(Q, peer).wait_recv()
-
-    each_peer(wait_small)
-
-    live, start, first = bounds[0], bounds[1], bounds[2]
-
-    def set_limit(d, _):
-        base = pl.multiple_of(d * ROWS, 8)
+        page(KEYS, peer).start()
+        page(VALUES, peer).start()
+
+    def near(i, _):
+        z = lax.rem(my_z + depth // 2 + i, depth)
+
+        @pl.when(z != my_z)
+        def _():
+            start_pages(z * 4 + my_y * 2 + my_c)
+            start_pages(z * 4 + my_y * 2 + (1 - my_c))
+
+        return 0
+
+    lax.fori_loop(0, depth, near, 0)
+
+    own_row(QROW).wait()
+    each(depth, my_z, lambda z: row(QROW, z, True).wait_recv())
+    q_y_out = qbuf.at[:, rows_of((my_c * 2 + my_y) * depth, depth), :]
+    q_y_in = qbuf.at[:, rows_of((my_c * 2 + 1 - my_y) * depth, depth), :]
+    pair(0, q_y_out, q_y_out, across).start()
+    pair(0, q_y_out, q_y_in, across).wait_recv()
+    q_c_out = qbuf.at[:, rows_of(my_c * 2 * depth, 2 * depth), :]
+    q_c_in = qbuf.at[:, rows_of((1 - my_c) * 2 * depth, 2 * depth), :]
+    pair(1, q_c_out, q_c_out, sibling).start()
+    own_page(META).wait()
+    each(n, me, lambda peer: page(META, peer, True).wait_recv())
+
+    live = PAGE * counts[me]
+    start = PAGE * lax.fori_loop(
+        0, n, lambda i, sofar: sofar + jnp.where(i < me, counts[i], 0), jnp.int32(0)
+    )
+    prompt = PAGE * lax.fori_loop(0, n, lambda i, sofar: sofar + counts[i], jnp.int32(0))
+
+    def set_limit(p, _):
+        d = (p % depth) * 4 + ((p // depth) % 2) * 2 + p // (2 * depth)
+        base = pl.multiple_of(p * ROWS, 8)
         context = jnp.broadcast_to(meta_out[d][:, 0:1], (8, LANES))
         reach = jnp.minimum(live, context - start)
-        limit[pl.ds(base, 8), :] = jnp.full((8, LANES), jnp.minimum(live, first + d + 1 - start))
+        limit[pl.ds(base, 8), :] = jnp.full(
+            (8, LANES), jnp.minimum(live, prompt - n + d + 1 - start)
+        )
         for s in range(STEPS):
             limit[pl.ds(pl.multiple_of(base + 8 * (s + 1), 8), 8), :] = reach
         return 0
 
     lax.fori_loop(0, n, set_limit, 0)
+    pair(1, q_c_out, q_c_in, sibling).wait_recv()
 
     lane = lax.broadcasted_iota(jnp.int32, (chunk, LANES), 1)
     keys = ck_ref.shape[0]
@@ -215,16 +255,44 @@
 
     lax.fori_loop(0, stat.shape[0] // chunk, attend, 0)
 
-    def start_parts(peer):
-        outgoing(STAT, peer).start()
-        outgoing(PART, peer).start()
-
-    each_peer(start_parts)
-    own(STAT).start()
-    own(PART).start()
+    def merge(a, a_stat, first, b, b_stat, to, to_stat):
+        step = 2 * ROWS
+
+        def some(i, _):
+            here = pl.ds(pl.multiple_of(i * step, 16), step)
+            there = pl.ds(pl.multiple_of(first * ROWS + i * step, 16), step)
+            one, two = a_stat[there, :], b_stat[here, :]
+            high = jnp.maximum(one, two)
+            one, two = jnp.exp(one - high), jnp.exp(two - high)
+            both = one + two
+            to_stat[here, :] = high + jnp.log(both)
+            one, two = one / both, two / both
+            for g in range(KVH):
+                to[g, here, :] = (
+                    one[:, g : g + 1] * a[g, there, :].astype(jnp.float32)
+                    + two[:, g : g + 1] * b[g, here, :].astype(jnp.float32)
+                ).astype(jnp.bfloat16)
+            return 0
+
+        lax.fori_loop(0, to_stat.shape[0] // step, some, 0)
+
+    give = (1 - my_c) * 2 * depth
+    part1 = pair(2, obuf.at[:, rows_of(give, 2 * depth), :], got1, sibling)
+    part1s = pair(3, stat.at[rows_of(give, 2 * depth), :], got1s, sibling)
+    part1s.start()
+    part1.start()
+    part1s.wait_recv()
+    part1.wait_recv()
+    merge(obuf, stat, my_c * 2 * depth, got1, got1s, obuf1, stat1)
+    give = (1 - my_y) * depth
+    part2 = pair(4, obuf1.at[:, rows_of(give, depth), :], got2, across)
+    part2s = pair(5, stat1.at[rows_of(give, depth), :], got2s, across)
+    part2s.start()
+    part2.start()
+    start_pages(sibling)
 
     own_lane = lax.broadcasted_iota(jnp.int32, (ROWS, LANES), 1)
-    own_row = lax.broadcasted_iota(jnp.int32, (ROWS, LANES), 0)
+    own_place = lax.broadcasted_iota(jnp.int32, (ROWS, LANES), 0)
     own_levels = []
     for t in range(STEPS):
         level = jnp.zeros((ROWS, LANES), jnp.float32)
@@ -232,19 +300,39 @@
             key = ok_ref[t : t + 1, g * HD : (g + 1) * HD].astype(jnp.float32)
             score = jnp.sum(q_ref[g].astype(jnp.float32) * key, axis=1, keepdims=True) * SCALE
             level = jnp.where(own_lane == g, score, level)
-        own_levels.append(jnp.where(own_row >= GROUP * (t + 1), level, MASKED))
-
-    own(STAT).wait()
-    own(PART).wait()
-
-    def wait_parts(peer):
-        incoming(STAT, peer).wait_recv()
-        incoming(PART, peer).wait_recv()
-
-    each_peer(wait_parts)
+        own_levels.append(jnp.where(own_place >= GROUP * (t + 1), level, MASKED))
+
+    part2s.wait_recv()
+    part2.wait_recv()
+    merge(obuf1, stat1, my_y * depth, got2, got2s, obuf2, stat2)
+
+    def start_rows(z):
+        row(STAT, z).start()
+        row(PART, z).start()
+
+    each(depth, my_z, start_rows)
+    own_row(STAT).start()
+    own_row(PART).start()
+
+    def far(i, _):
+        z = lax.rem(my_z + depth // 2 + i, depth)
+        start_pages(z * 4 + (1 - my_y) * 2 + my_c)
+        start_pages(z * 4 + (1 - my_y) * 2 + (1 - my_c))
+        return 0
+
+    lax.fori_loop(0, depth, far, 0)
+
+    own_row(STAT).wait()
+    own_row(PART).wait()
+
+    def wait_rows(z):
+        row(STAT, z, True).wait_recv()
+        row(PART, z, True).wait_recv()
+
+    each(depth, my_z, wait_rows)
 
     top = functools.reduce(jnp.maximum, own_levels)
-    top = lax.fori_loop(0, n, lambda d, high: jnp.maximum(high, sbuf[d]), top)
+    top = lax.fori_loop(0, depth, lambda d, high: jnp.maximum(high, sbuf[d]), top)
 
     norm = jnp.zeros((ROWS, LANES), jnp.float32)
     sums = [jnp.zeros((ROWS, HD), jnp.float32) for _ in range(KVH)]
@@ -263,28 +351,46 @@
         )
         return norm + factor, sums
 
-    norm, sums = lax.fori_loop(0, n, add, (norm, tuple(sums)))
+    norm, sums = lax.fori_loop(0, depth, add, (norm, tuple(sums)))
     for g in range(KVH):
         out_ref[g] = (sums[g] / norm[:, g : g + 1]).astype(out_ref.dtype)
 
-    own(KEYS).wait()
-    own(VALUES).wait()
+    pair(0, q_y_out, q_y_out, across).wait_send()
+    pair(1, q_c_out, q_c_out, sibling).wait_send()
+    for copy in (part1, part1s, part2, part2s):
+        copy.wait_send()
+
+    def finish_row(z):
+        for kind in (QROW, PART, STAT):
+            row(kind, z).wait_send()
+
+    each(depth, my_z, finish_row)
+    own_page(KEYS).wait()
+    own_page(VALUES).wait()
 
     def finish(peer):
-        incoming(KEYS, peer).wait_recv()
-        incoming(VALUES, peer).wait_recv()
-        for kind in (Q, META, KEYS, VALUES, PART, STAT):
-            outgoing(kind, peer).wait_send()
-
-    each_peer(finish)
-
-
-def main(n, cap, bounds, q, meta, ck, cv, pk, pv, own_k, own_v):
+        page(KEYS, peer, True).wait_recv()
+        page(VALUES, peer, True).wait_recv()
+        for kind in (META, KEYS, VALUES):
+            page(kind, peer).wait_send()
+
+    each(n, me, finish)
+
+
+def main(n, cap, counts, q, meta, ck, cv, pk, pv, own_k, own_v):
     height = n * ROWS
     chunk = min(height, 384)
     vmem = pl.BlockSpec(memory_space=pltpu.VMEM)
     smem = pl.BlockSpec(memory_space=pltpu.SMEM)
     hbm = pl.BlockSpec(memory_space=pl.ANY)
+
+    def parts(rows):
+        return pltpu.VMEM((KVH, rows, HD), jnp.bfloat16)
+
+    def stats(rows):
+        return pltpu.VMEM((rows, LANES), jnp.float32)
+
+    half, quarter, depth = height // 2, height // 4, n // 4
     return pl.pallas_call(
         functools.partial(main_kernel, n, cap, chunk),
         in_specs=[smem, vmem, vmem, vmem, vmem, hbm, hbm, vmem, vmem],
@@ -296,21 +402,24 @@
             jax.ShapeDtypeStruct(meta.shape, meta.dtype),
         ),
         scratch_shapes=[
-            pltpu.VMEM((KVH, height, HD), jnp.bfloat16),
-            pltpu.VMEM((KVH, height, HD), jnp.bfloat16),
-            pltpu.VMEM((height, LANES), jnp.float32),
-            pltpu.VMEM((height, LANES), jnp.int32),
-            pltpu.VMEM((n, KVH, ROWS, HD), jnp.bfloat16),
-            pltpu.VMEM((n, ROWS, LANES), jnp.float32),
-            pltpu.SemaphoreType.DMA((6, n)),
-            pltpu.SemaphoreType.DMA((6, n)),
+            parts(height), parts(height), stats(height), pltpu.VMEM((height, LANES), jnp.int32),
+            parts(half), stats(half), parts(half), stats(half),
+            parts(quarter), stats(quarter), parts(quarter), stats(quarter),
+            pltpu.VMEM((depth, KVH, ROWS, HD), jnp.bfloat16),
+            pltpu.VMEM((depth, ROWS, LANES), jnp.float32),
+            pltpu.SemaphoreType.DMA((3, n)),
+            pltpu.SemaphoreType.DMA((3, n)),
+            pltpu.SemaphoreType.DMA((3, depth)),
+            pltpu.SemaphoreType.DMA((3, depth)),
+            pltpu.SemaphoreType.DMA((6,)),
+            pltpu.SemaphoreType.DMA((6,)),
             pltpu.SemaphoreType.DMA((6,)),
         ],
         compiler_params=pltpu.CompilerParams(
             collective_id=0, has_side_effects=True, vmem_limit_bytes=48 << 20
         ),
         name="exchange",
-    )(bounds, q, meta, ck, cv, pk, pv, own_k, own_v)
+    )(counts, q, meta, ck, cv, pk, pv, own_k, own_v)
 
 
 def per_device(
@@ -323,18 +432,10 @@
     ck = cache_k.reshape(page_slots, PAGE, KVD)
     cv = cache_v.reshape(page_slots, PAGE, KVD)
     pk, pv, meta = pack(n, cap, page_owner[:, 0], page_counts, context_len, ck, cv)
-    position = jnp.arange(n, dtype=jnp.int32)
-    bounds = PAGE * jnp.stack(
-        [
-            jnp.sum(jnp.where(position == me, page_counts, 0)),
-            jnp.sum(jnp.where(position < me, page_counts, 0)),
-            jnp.sum(page_counts),
-        ]
-    ) - jnp.array([0, 0, n], jnp.int32)
     q = jnp.concatenate((prefill_q, decode_q[0]), axis=0)
     q = q.reshape(1 + STEPS, KVH, GROUP, HD).transpose(1, 0, 2, 3).reshape(KVH, ROWS, HD)
     out, store_k, store_v, meta = main(
-        n, cap, bounds, q, meta, cache_k, cache_v, pk, pv, decode_k[0], decode_v[0]
+        n, cap, page_counts, q, meta, cache_k, cache_v, pk, pv, decode_k[0], decode_v[0]
     )
     out = out.reshape(KVH, 1 + STEPS, GROUP, HD).transpose(1, 0, 2, 3).reshape(1 + STEPS, HQ * HD)
     return (

time: 166 us -> 135 us (0.81)
  Pallas kernels: 149 us -> 122 us
  other arithmetic: 5.62 us -> 1.62 us
    pallas_call x1, Pallas kernels: 140 us -> 112 us  [main(): pl.pallas_call(functools.partial(main_kernel, n, cap, chunk), in_specs=[s...]
    sub x1 -> x0, other arithmetic: 2.67 us -> none  [per_device(): PAGE * jnp.stack([jnp.sum(jnp.where(position == me, page_counts, 0)), jnp...]
    unnamed x16 -> x18, local copies, waits for them, and re-layouts: 6.72 us -> 6.72 us
where the time goes in v2:
time: 135 us; the launch traced here: 134 us
  Pallas kernels  122 us (90%)
  local copies, waits for them, and re-layouts  9.01 us (7%)
  other arithmetic  1.62 us (1%)
  between operations  1.53 us (1%)
    pallas_call x1, Pallas kernels, main(): pl.pallas_call(functools.partial(main_kernel, n, cap, chunk), in_specs=[s...  112 us
    pallas_call x1, Pallas kernels, pack(): pl.pallas_call(functools.partial(pack_kernel, n, cap, page_slots), grid=(...  10 us
    unnamed x18, local copies, waits for them, and re-layouts  6.72 us

profile of v2, /device:TPU:15, one launch (start us, length us, event | category | flops | bytes accessed | tf_op | source)
XLA Modules:
  0.0 134.0 jit_solution(16570730809790046175)
XLA Ops:
  0.6 0.0 copy-start.6
  0.6 0.0 copy-start.1
  0.7 0.0 copy-start
  0.7 0.0 copy-start.5
  0.7 0.0 copy-start.4
  1.5 0.8 reduce
  2.3 0.8 maximum_bitcast_fusion.q_ref
  3.1 10.0 %pack.1 = (bf16[128,8,1024]{2,1,0:T(8,128)(2,1)}, bf16[128,8,1024]{2,1,0:T(8,128)(2,1)}, s32[16,8,128]{2,1,0:T(8,128)}) custom-call(s32[64]{0:T(128)} %bitcast.40, s32[16]{0:T(128)} %counts.3, s32[1]{0:T(128)S(6)} %copy.28.context, bf16[64,8,1024]{2,1,0:T(8,128)(2,1)} %bitcast.30, bf16[64,8,1024]{2,1,0:T(8,128)(2,1)} %bitcast.31), custom_call_target="tpu_custom_call" | custom-call | tf_op jit(solution)/shard_map/pack/pallas_call | solution.py:80
  13.1 0.0 copy-done.6
  13.1 0.0 copy-done.1
  13.1 0.0 copy-done
  13.1 0.0 copy-done.5
  13.1 0.0 copy-done.4
  13.2 0.0 copy-start.3
  13.2 0.8 copy-done.3
  14.0 111.9 %exchange.1 = (bf16[8,24,128]{2,1,0:T(8,128)(2,1)S(1)}, bf16[128,8,1024]{2,1,0:T(8,128)(2,1)S(1)}, bf16[128,8,1024]{2,1,0:T(8,128)(2,1)}, s32[16,8,128]{2,1,0:T(8,128)S(1)}) custom-call(s32[16]{0:T(128)S(1)} %copy-done.6, bf16[8,24,128]{2,1,0:T(8,128)(2,1)S(1)} %maximum_bitcast_fusion.q_ref, s32[16,8,128]{2,1,0:T(8,128)S(1)} %copy-done.3, ...), custom_call_target="tpu_custom_call" | custom-call | tf_op jit(solution)/shard_map/exchange/pallas_call | solution.py:394
  125.9 0.0 copy-start.2
  125.9 1.3 copy-done.2
  127.2 0.4 slice_reduce_fusion
  127.6 0.6 reshape_squeeze.3
  128.2 0.6 reshape.43
  128.9 0.6 slice.14
  129.5 0.0 copy-start.7
  129.5 3.2 %copy.29 = bf16[1024,1024]{1,0:T(8,128)(2,1)} copy(bf16[1024,1024]{1,0:T(8,128)(2,1)} %bitcast.32) | data formatting | bytes 4194304
  132.7 0.0 copy-done.7
  132.7 1.3 copy.30
  (3 shorter events, 0.0 us)
Async XLA Ops:
  0.6 12.5 %copy-start.6 = (s32[16]{0:T(128)S(1)}, s32[16]{0:T(128)}, u32[]{:S(2)}) copy-start(s32[16]{0:T(128)} %counts.3) | copy-start | bytes 196
  0.6 12.5 %copy-start.1 = (bf16[512,1024]{1,0:T(8,128)(2,1)S(1)}, bf16[512,1024]{1,0:T(8,128)(2,1)}, u32[]{:S(2)}) copy-start(bf16[512,1024]{1,0:T(8,128)(2,1)} %cv_ref.1) | copy-start | bytes 3145732
  0.7 12.5 %copy-start = (bf16[512,1024]{1,0:T(8,128)(2,1)S(1)}, bf16[512,1024]{1,0:T(8,128)(2,1)}, u32[]{:S(2)}) copy-start(bf16[512,1024]{1,0:T(8,128)(2,1)} %ck_ref.1) | copy-start | bytes 3145732
  0.7 12.5 %copy-start.5 = (bf16[1,2,1024]{2,1,0:T(2,128)(2,1)S(1)}, bf16[1,2,1024]{2,1,0:T(2,128)(2,1)}, u32[]{:S(2)}) copy-start(bf16[1,2,1024]{2,1,0:T(2,128)(2,1)} %param.16) | copy-start | bytes 12292
  0.7 12.5 %copy-start.4 = (bf16[1,2,1024]{2,1,0:T(2,128)(2,1)S(1)}, bf16[1,2,1024]{2,1,0:T(2,128)(2,1)}, u32[]{:S(2)}) copy-start(bf16[1,2,1024]{2,1,0:T(2,128)(2,1)} %param.15) | copy-start | bytes 12292
  13.2 0.8 copy-start.3
  125.9 1.3 copy-start.2
  129.5 3.2 %copy-start.7 = (bf16[128,8,1024]{2,1,0:T(8,128)(2,1)S(1)}, bf16[128,8,1024]{2,1,0:T(8,128)(2,1)}, u32[]{:S(2)}) copy-start(bf16[128,8,1024]{2,1,0:T(8,128)(2,1)} %get-tuple-element.17) | copy-start | bytes 6291460

commit v3 on v2

--- a/solution.py
+++ b/solution.py
@@ -26,68 +26,59 @@
 
 
 def pack_kernel(n, cap, page_slots, owner, counts, context, ck, cv, out_k, out_v, meta, table, seen):
-    dst = pl.program_id(0)
     me = lax.axis_index("seq")
 
-    @pl.when(dst == 0)
-    def _():
-        def clear(i, _):
-            table[i] = -1
-            return 0
-
-        lax.fori_loop(0, n * cap, clear, 0)
-
-        def clear_seen(i, _):
-            seen[i] = 0
-            return 0
-
-        lax.fori_loop(0, n, clear_seen, 0)
-
-        def place(j, _):
-            o = owner[j]
-            k = seen[o]
-            seen[o] = k + 1
-            table[o * cap + k] = j
-            return 0
-
-        lax.fori_loop(0, counts[me], place, 0)
+    def clear(i, _):
+        seen[i] = 0
+        for k in range(cap):
+            table[i * cap + k] = -1
+        return 0
+
+    lax.fori_loop(0, n, clear, 0)
+
+    def place(j, _):
+        o = owner[j]
+        k = seen[o]
+        seen[o] = k + 1
+        table[o * cap + k] = j
+        return 0
+
+    lax.fori_loop(0, counts[me], place, 0)
 
     tile_row = lax.broadcasted_iota(jnp.int32, (8, LANES), 0)
-    ids = jnp.full((8, LANES), -1, jnp.int32)
-    for k in range(cap):
-        src = table[dst * cap + k]
-        ids = jnp.where(tile_row == k, jnp.where(src >= 0, me * page_slots + src, -1), ids)
-
-        @pl.when(src >= 0)
-        def _():
-            out_k[k] = ck[src]
-            out_v[k] = cv[src]
-
-        @pl.when(src < 0)
-        def _():
-            out_k[k] = jnp.zeros((PAGE, KVD), out_k.dtype)
-            out_v[k] = jnp.zeros((PAGE, KVD), out_v.dtype)
-
     lane = lax.broadcasted_iota(jnp.int32, (8, LANES), 1)
-    meta[0] = jnp.where(lane < ID_LANE, context[0], ids)
+
+    def fill(dst, _):
+        ids = jnp.full((8, LANES), -1, jnp.int32)
+        for k in range(cap):
+            slot = dst * cap + k
+            src = table[slot]
+            page = jnp.maximum(src, 0)
+            there = jnp.full((PAGE, KVD), src, jnp.int32) >= 0
+            out_k[slot] = jnp.where(there, ck[page], jnp.zeros((), out_k.dtype))
+            out_v[slot] = jnp.where(there, cv[page], jnp.zeros((), out_v.dtype))
+            ids = jnp.where(tile_row == k, jnp.where(src >= 0, me * page_slots + src, -1), ids)
+        meta[dst] = jnp.where(lane < ID_LANE, context[0], ids)
+        return 0
+
+    lax.fori_loop(0, n, fill, 0)
 
 
 def pack(n, cap, owner, counts, context, ck, cv):
     page_slots = ck.shape[0]
     smem = pl.BlockSpec(memory_space=pltpu.SMEM)
-    whole = pl.BlockSpec(ck.shape, lambda d: (0, 0, 0))
-    block = pl.BlockSpec((cap, PAGE, KVD), lambda d: (d, 0, 0))
+    vmem = pl.BlockSpec(memory_space=pltpu.VMEM)
     return pl.pallas_call(
         functools.partial(pack_kernel, n, cap, page_slots),
-        grid=(n,),
-        in_specs=[smem, smem, smem, whole, whole],
-        out_specs=(block, block, pl.BlockSpec((1, 8, LANES), lambda d: (d, 0, 0))),
+        in_specs=[smem, smem, smem, vmem, vmem],
+        out_specs=(vmem, vmem, vmem),
         out_shape=(
             jax.ShapeDtypeStruct((n * cap, PAGE, KVD), ck.dtype),
             jax.ShapeDtypeStruct((n * cap, PAGE, KVD), cv.dtype),
             jax.ShapeDtypeStruct((n, 8, LANES), jnp.int32),
         ),
         scratch_shapes=[pltpu.SMEM((n * cap,), jnp.int32), pltpu.SMEM((n,), jnp.int32)],
+        compiler_params=pltpu.CompilerParams(vmem_limit_bytes=16 << 20),
         name="pack",
     )(owner, counts, context, ck, cv)
 
@@ -382,7 +373,6 @@
     chunk = min(height, 384)
     vmem = pl.BlockSpec(memory_space=pltpu.VMEM)
     smem = pl.BlockSpec(memory_space=pltpu.SMEM)
-    hbm = pl.BlockSpec(memory_space=pl.ANY)
 
     def parts(rows):
         return pltpu.VMEM((KVH, rows, HD), jnp.bfloat16)
@@ -393,8 +383,8 @@
     half, quarter, depth = height // 2, height // 4, n // 4
     return pl.pallas_call(
         functools.partial(main_kernel, n, cap, chunk),
-        in_specs=[smem, vmem, vmem, vmem, vmem, hbm, hbm, vmem, vmem],
-        out_specs=(vmem, hbm, hbm, vmem),
+        in_specs=[smem] + [vmem] * 8,
+        out_specs=(vmem, vmem, vmem, vmem),
         out_shape=(
             jax.ShapeDtypeStruct((KVH, ROWS, HD), jnp.bfloat16),
             jax.ShapeDtypeStruct(pk.shape, pk.dtype),
@@ -416,10 +406,38 @@
             pltpu.SemaphoreType.DMA((6,)),
         ],
         compiler_params=pltpu.CompilerParams(
-            collective_id=0, has_side_effects=True, vmem_limit_bytes=48 << 20
+            collective_id=0, has_side_effects=True, vmem_limit_bytes=32 << 20
         ),
         name="exchange",
     )(counts, q, meta, ck, cv, pk, pv, own_k, own_v)
+
+
+def write_kernel(k_in, v_in, k_out, v_out, done):
+    copies = [
+        pltpu.make_async_copy(k_in, k_out, done.at[0]),
+        pltpu.make_async_copy(v_in, v_out, done.at[1]),
+    ]
+    for copy in copies:
+        copy.start()
+    for copy in copies:
+        copy.wait()
+
+
+def write(store_k, store_v):
+    vmem = pl.BlockSpec(memory_space=pltpu.VMEM)
+    hbm = pl.BlockSpec(memory_space=pl.ANY)
+    return pl.pallas_call(
+        write_kernel,
+        in_specs=[vmem, vmem],
+        out_specs=(hbm, hbm),
+        out_shape=(
+            jax.ShapeDtypeStruct(store_k.shape, store_k.dtype),
+            jax.ShapeDtypeStruct(store_v.shape, store_v.dtype),
+        ),
+        scratch_shapes=[pltpu.SemaphoreType.DMA((2,))],
+        compiler_params=pltpu.CompilerParams(vmem_limit_bytes=16 << 20),
+        name="write",
+    )(store_k, store_v)
 
 
 def per_device(
@@ -437,6 +455,8 @@
     out, store_k, store_v, meta = main(
         n, cap, page_counts, q, meta, cache_k, cache_v, pk, pv, decode_k[0], decode_v[0]
     )
+    store_k, store_v = write(store_k, store_v)
+    store_k, store_v, out, meta = lax.optimization_barrier((store_k, store_v, out, meta))
     out = out.reshape(KVH, 1 + STEPS, GROUP, HD).transpose(1, 0, 2, 3).reshape(1 + STEPS, HQ * HD)
     return (
         out[:1],

time: 135 us -> 126 us (0.933)
  Pallas kernels: 122 us -> 116 us
  local copies, waits for them, and re-layouts: 9.01 us -> 6.07 us
    pallas_call x1 -> x2, Pallas kernels: 10 us -> 4.29 us  [the longest x1 2.27 us: pack(): pl.pallas_call(functools.partial(pack_kernel, n, cap, page_slots), in_spe...]
    unnamed x18, local copies, waits for them, and re-layouts: 6.72 us -> 3.78 us
where the time goes in v3:
time: 126 us; the launch traced here: 125 us
  Pallas kernels  116 us (92%)
  local copies, waits for them, and re-layouts  6.07 us (5%)
  other arithmetic  1.62 us (1%)
  between operations  1.41 us (1%)
    pallas_call x1, Pallas kernels, main(): pl.pallas_call(functools.partial(main_kernel, n, cap, chunk), in_specs=[s...  112 us
    unnamed x18, local copies, waits for them, and re-layouts  3.78 us

profile of v3, /device:TPU:15, one launch (start us, length us, event | category | flops | bytes accessed | tf_op | source)
XLA Modules:
  0.0 125.4 jit_solution(275692487410897324)
XLA Ops:
  0.6 0.0 copy-start.7
  0.6 0.0 copy-start.5
  0.7 0.0 copy-start.4
  1.3 0.8 reduce
  2.2 0.8 maximum_bitcast_fusion.q_ref
  3.0 0.0 copy-start
  3.0 1.2 copy-done
  4.2 0.0 copy-start.2
  4.2 1.2 copy-done.2
  5.4 0.0 copy-start.6
  5.4 0.7 copy-done.6
  6.1 0.0 copy-start.8
  6.1 0.7 copy-done.8
  6.7 0.0 copy-start.1
  6.7 0.0 copy-start.3
  6.7 2.3 %pack.1 = (bf16[128,8,1024]{2,1,0:T(8,128)(2,1)S(1)}, bf16[128,8,1024]{2,1,0:T(8,128)(2,1)S(1)}, s32[16,8,128]{2,1,0:T(8,128)S(1)}) custom-call(s32[64]{0:T(128)S(1)} %bitcast.36, s32[16]{0:T(128)S(1)} %copy-done.6, s32[1]{0:T(128)S(6)} %copy.26.context, bf16[64,8,1024]{2,1,0:T(8,128)(2,1)S(1)} %bitcast.30, bf16[64,8,1024]{2,1,0:T(8,128)(2,1)S(1)} %bitcast.31), custom_call_target="tpu_custom_call" | custom-call | tf_op jit(solution)/shard_map/pack/pallas_call | solution.py:71
  9.0 0.0 copy-done.7
  9.0 0.0 copy-done.5
  9.0 0.0 copy-done.4
  9.0 0.0 copy-done.1
  9.0 0.0 copy-done.3
  9.1 112.0 %exchange.1 = (bf16[8,24,128]{2,1,0:T(8,128)(2,1)S(1)}, bf16[128,8,1024]{2,1,0:T(8,128)(2,1)S(1)}, bf16[128,8,1024]{2,1,0:T(8,128)(2,1)S(1)}, s32[16,8,128]{2,1,0:T(8,128)S(1)}) custom-call(s32[16]{0:T(128)S(1)} %copy-done.7, bf16[8,24,128]{2,1,0:T(8,128)(2,1)S(1)} %maximum_bitcast_fusion.q_ref, s32[16,8,128]{2,1,0:T(8,128)S(1)} %get-tuple-element.18.meta_ref, ...), custom_call_target="tpu_custom_call" | custom-call | tf_op jit(solution)/shard_map/exchange/pallas_call | solution.py:384
  121.0 2.0 %write.1 = (bf16[128,8,1024]{2,1,0:T(8,128)(2,1)}, bf16[128,8,1024]{2,1,0:T(8,128)(2,1)}) custom-call(bf16[128,8,1024]{2,1,0:T(8,128)(2,1)S(1)} %get-tuple-element.21.k_in, bf16[128,8,1024]{2,1,0:T(8,128)(2,1)S(1)} %get-tuple-element.22.v_in), custom_call_target="tpu_custom_call" | custom-call | tf_op jit(solution)/shard_map/write/pallas_call | solution.py:429
  123.1 0.4 slice_reduce_fusion
  123.5 0.6 reshape_squeeze.3
  124.1 0.6 reshape.43
  124.7 0.6 slice.14
  (3 shorter events, 0.0 us)
Async XLA Ops:
  0.6 8.4 %copy-start.7 = (s32[16]{0:T(128)S(1)}, s32[16]{0:T(128)}, u32[]{:S(2)}) copy-start(s32[16]{0:T(128)} %counts.3) | copy-start | bytes 196
  0.6 8.4 %copy-start.5 = (bf16[1,2,1024]{2,1,0:T(2,128)(2,1)S(1)}, bf16[1,2,1024]{2,1,0:T(2,128)(2,1)}, u32[]{:S(2)}) copy-start(bf16[1,2,1024]{2,1,0:T(2,128)(2,1)} %param.16) | copy-start | bytes 12292
  0.7 8.4 %copy-start.4 = (bf16[1,2,1024]{2,1,0:T(2,128)(2,1)S(1)}, bf16[1,2,1024]{2,1,0:T(2,128)(2,1)}, u32[]{:S(2)}) copy-start(bf16[1,2,1024]{2,1,0:T(2,128)(2,1)} %param.15) | copy-start | bytes 12292
  3.0 1.2 copy-start
  4.2 1.2 copy-start.2
  5.4 0.7 copy-start.6
  6.1 0.7 copy-start.8
  6.7 2.3 %copy-start.1 = (bf16[512,1024]{1,0:T(8,128)(2,1)S(1)}, bf16[512,1024]{1,0:T(8,128)(2,1)}, u32[]{:S(2)}) copy-start(bf16[512,1024]{1,0:T(8,128)(2,1)} %ck_ref.1) | copy-start | bytes 3145732
  6.7 2.3 %copy-start.3 = (bf16[512,1024]{1,0:T(8,128)(2,1)S(1)}, bf16[512,1024]{1,0:T(8,128)(2,1)}, u32[]{:S(2)}) copy-start(bf16[512,1024]{1,0:T(8,128)(2,1)} %cv_ref.1) | copy-start | bytes 3145732

commit v4 on v3

--- a/solution.py
+++ b/solution.py
@@ -25,8 +25,17 @@
 QROW, PART, STAT = range(3)
 
 
-def pack_kernel(n, cap, page_slots, owner, counts, context, ck, cv, out_k, out_v, meta, table, seen):
+def pack_kernel(
+    n, cap, page_slots, owner, counts, context, ck_hbm, cv_hbm, out_k, out_v, meta,
+    ck, cv, table, seen, done,
+):
     me = lax.axis_index("seq")
+    loads = [
+        pltpu.make_async_copy(ck_hbm, ck, done.at[0]),
+        pltpu.make_async_copy(cv_hbm, cv, done.at[1]),
+    ]
+    for load in loads:
+        load.start()
 
     def clear(i, _):
         seen[i] = 0
@@ -44,6 +53,9 @@
         return 0
 
     lax.fori_loop(0, counts[me], place, 0)
+
+    for load in loads:
+        load.wait()
 
     tile_row = lax.broadcasted_iota(jnp.int32, (8, LANES), 0)
     lane = lax.broadcasted_iota(jnp.int32, (8, LANES), 1)
@@ -68,16 +80,21 @@
     page_slots = ck.shape[0]
     smem = pl.BlockSpec(memory_space=pltpu.SMEM)
     vmem = pl.BlockSpec(memory_space=pltpu.VMEM)
+    hbm = pl.BlockSpec(memory_space=pl.ANY)
     return pl.pallas_call(
         functools.partial(pack_kernel, n, cap, page_slots),
-        in_specs=[smem, smem, smem, vmem, vmem],
+        in_specs=[smem, smem, smem, hbm, hbm],
         out_specs=(vmem, vmem, vmem),
         out_shape=(
             jax.ShapeDtypeStruct((n * cap, PAGE, KVD), ck.dtype),
             jax.ShapeDtypeStruct((n * cap, PAGE, KVD), cv.dtype),
             jax.ShapeDtypeStruct((n, 8, LANES), jnp.int32),
         ),
-        scratch_shapes=[pltpu.SMEM((n * cap,), jnp.int32), pltpu.SMEM((n,), jnp.int32)],
+        scratch_shapes=[
+            pltpu.VMEM(ck.shape, ck.dtype), pltpu.VMEM(cv.shape, cv.dtype),
+            pltpu.SMEM((n * cap,), jnp.int32), pltpu.SMEM((n,), jnp.int32),
+            pltpu.SemaphoreType.DMA((2,)),
+        ],
         compiler_params=pltpu.CompilerParams(vmem_limit_bytes=16 << 20),
         name="pack",
     )(owner, counts, context, ck, cv)
@@ -215,6 +232,14 @@
 
     lax.fori_loop(0, n, set_limit, 0)
     pair(1, q_c_out, q_c_in, sibling).wait_recv()
+
+    def far(i, _):
+        z = lax.rem(my_z + depth // 2 + i, depth)
+        start_pages(z * 4 + (1 - my_y) * 2 + my_c)
+        start_pages(z * 4 + (1 - my_y) * 2 + (1 - my_c))
+        return 0
+
+    far(0, 0)
 
     lane = lax.broadcasted_iota(jnp.int32, (chunk, LANES), 1)
     keys = ck_ref.shape[0]
@@ -305,13 +330,7 @@
     own_row(STAT).start()
     own_row(PART).start()
 
-    def far(i, _):
-        z = lax.rem(my_z + depth // 2 + i, depth)
-        start_pages(z * 4 + (1 - my_y) * 2 + my_c)
-        start_pages(z * 4 + (1 - my_y) * 2 + (1 - my_c))
-        return 0
-
-    lax.fori_loop(0, depth, far, 0)
+    lax.fori_loop(1, depth, far, 0)
 
     own_row(STAT).wait()
     own_row(PART).wait()

time: 126 us -> 122 us (0.968)
  Pallas kernels: 116 us -> 112 us
    pallas_call x1, Pallas kernels: 112 us -> 108 us  [main(): pl.pallas_call(functools.partial(main_kernel, n, cap, chunk), in_specs=[s...]
where the time goes in v4:
time: 122 us
  Pallas kernels  112 us (92%)
  local copies, waits for them, and re-layouts  6.07 us (5%)
  other arithmetic  1.62 us (1%)
  between operations  1.41 us (1%)
    pallas_call x1, Pallas kernels, main(): pl.pallas_call(functools.partial(main_kernel, n, cap, chunk), in_specs=[s...  108 us
    unnamed x18, local copies, waits for them, and re-layouts  3.78 us

profile of v4, /device:TPU:15, one launch (start us, length us, event | category | flops | bytes accessed | tf_op | source)
XLA Modules:
  0.0 121.5 jit_solution(16284235956888986547)
XLA Ops:
  0.6 0.0 copy-start.7
  0.6 0.0 copy-start.5
  0.7 0.0 copy-start.4
  1.3 0.8 reduce
  2.2 0.8 maximum_bitcast_fusion.q_ref
  3.0 0.0 copy-start
  3.0 1.2 %copy-done = bf16[512,1024]{1,0:T(8,128)(2,1)S(1)} copy-done((bf16[512,1024]{1,0:T(8,128)(2,1)S(1)}, bf16[512,1024]{1,0:T(8,128)(2,1)}, u32[]{:S(2)}) %copy-start) | copy-done | bytes 1048600
  4.2 0.0 copy-start.2
  4.2 1.2 %copy-done.2 = bf16[512,1024]{1,0:T(8,128)(2,1)S(1)} copy-done((bf16[512,1024]{1,0:T(8,128)(2,1)S(1)}, bf16[512,1024]{1,0:T(8,128)(2,1)}, u32[]{:S(2)}) %copy-start.2) | copy-done | bytes 1048600
  5.4 0.0 copy-start.6
  5.4 0.7 copy-done.6
  6.1 0.0 copy-start.8
  6.1 0.7 copy-done.8
  6.7 0.0 copy-start.1
  6.7 0.0 copy-start.3
  6.7 2.4 %pack.1 = (bf16[128,8,1024]{2,1,0:T(8,128)(2,1)S(1)}, bf16[128,8,1024]{2,1,0:T(8,128)(2,1)S(1)}, s32[16,8,128]{2,1,0:T(8,128)S(1)}) custom-call(s32[64]{0:T(128)S(1)} %bitcast.36, s32[16]{0:T(128)S(1)} %copy-done.6, s32[1]{0:T(128)S(6)} %copy.26.context, bf16[64,8,1024]{2,1,0:T(8,128)(2,1)S(1)} %bitcast.30, bf16[64,8,1024]{2,1,0:T(8,128)(2,1)S(1)} %bitcast.31), custom_call_target="tpu_custom_call" | custom-call | tf_op jit(solution)/shard_map/pack/pallas_call | solution.py:84
  9.1 0.0 copy-done.7
  9.1 0.0 copy-done.5
  9.2 0.0 copy-done.4
  9.2 0.0 copy-done.1
  9.2 0.0 copy-done.3
  9.2 108.0 %exchange.1 = (bf16[8,24,128]{2,1,0:T(8,128)(2,1)S(1)}, bf16[128,8,1024]{2,1,0:T(8,128)(2,1)S(1)}, bf16[128,8,1024]{2,1,0:T(8,128)(2,1)S(1)}, s32[16,8,128]{2,1,0:T(8,128)S(1)}) custom-call(s32[16]{0:T(128)S(1)} %copy-done.7, bf16[8,24,128]{2,1,0:T(8,128)(2,1)S(1)} %maximum_bitcast_fusion.q_ref, s32[16,8,128]{2,1,0:T(8,128)S(1)} %get-tuple-element.18.meta_ref, ...), custom_call_target="tpu_custom_call" | custom-call | tf_op jit(solution)/shard_map/exchange/pallas_call | solution.py:403
  117.2 2.0 %write.1 = (bf16[128,8,1024]{2,1,0:T(8,128)(2,1)}, bf16[128,8,1024]{2,1,0:T(8,128)(2,1)}) custom-call(bf16[128,8,1024]{2,1,0:T(8,128)(2,1)S(1)} %get-tuple-element.21.k_in, bf16[128,8,1024]{2,1,0:T(8,128)(2,1)S(1)} %get-tuple-element.22.v_in), custom_call_target="tpu_custom_call" | custom-call | tf_op jit(solution)/shard_map/write/pallas_call | solution.py:448
  119.2 0.4 slice_reduce_fusion
  119.6 0.6 reshape_squeeze.3
  120.3 0.6 reshape.43
  120.9 0.6 slice.14
  (3 shorter events, 0.0 us)
Async XLA Ops:
  0.6 8.5 %copy-start.7 = (s32[16]{0:T(128)S(1)}, s32[16]{0:T(128)}, u32[]{:S(2)}) copy-start(s32[16]{0:T(128)} %counts.3) | copy-start | bytes 196
  0.6 8.5 %copy-start.5 = (bf16[1,2,1024]{2,1,0:T(2,128)(2,1)S(1)}, bf16[1,2,1024]{2,1,0:T(2,128)(2,1)}, u32[]{:S(2)}) copy-start(bf16[1,2,1024]{2,1,0:T(2,128)(2,1)} %param.16) | copy-start | bytes 12292
  0.7 8.5 %copy-start.4 = (bf16[1,2,1024]{2,1,0:T(2,128)(2,1)S(1)}, bf16[1,2,1024]{2,1,0:T(2,128)(2,1)}, u32[]{:S(2)}) copy-start(bf16[1,2,1024]{2,1,0:T(2,128)(2,1)} %param.15) | copy-start | bytes 12292
  3.0 1.2 %copy-start = (bf16[512,1024]{1,0:T(8,128)(2,1)S(1)}, bf16[512,1024]{1,0:T(8,128)(2,1)}, u32[]{:S(2)}) copy-start(bf16[512,1024]{1,0:T(8,128)(2,1)} %ck_ref.1) | copy-start | bytes 3145732
  4.2 1.2 %copy-start.2 = (bf16[512,1024]{1,0:T(8,128)(2,1)S(1)}, bf16[512,1024]{1,0:T(8,128)(2,1)}, u32[]{:S(2)}) copy-start(bf16[512,1024]{1,0:T(8,128)(2,1)} %cv_ref.1) | copy-start | bytes 3145732
  5.4 0.7 copy-start.6
  6.1 0.7 copy-start.8
  6.7 2.4 %copy-start.1 = (bf16[512,1024]{1,0:T(8,128)(2,1)S(1)}, bf16[512,1024]{1,0:T(8,128)(2,1)}, u32[]{:S(2)}) copy-start(bf16[512,1024]{1,0:T(8,128)(2,1)} %ck_ref.1) | copy-start | bytes 3145732
  6.7 2.4 %copy-start.3 = (bf16[512,1024]{1,0:T(8,128)(2,1)S(1)}, bf16[512,1024]{1,0:T(8,128)(2,1)}, u32[]{:S(2)}) copy-start(bf16[512,1024]{1,0:T(8,128)(2,1)} %cv_ref.1) | copy-start | bytes 3145732

commit v5 on v4

--- a/solution.py
+++ b/solution.py
@@ -240,6 +240,7 @@
         return 0
 
     far(0, 0)
+    far(1, 0)
 
     lane = lax.broadcasted_iota(jnp.int32, (chunk, LANES), 1)
     keys = ck_ref.shape[0]
@@ -330,7 +331,7 @@
     own_row(STAT).start()
     own_row(PART).start()
 
-    lax.fori_loop(1, depth, far, 0)
+    lax.fori_loop(2, depth, far, 0)
 
     own_row(STAT).wait()
     own_row(PART).wait()

time: 122 us -> 124 us (1.016); the launches traced: 122 us -> 121 us
  no operation moved by 1% of the time
where the time goes in v5:
time: 124 us; the launch traced here: 121 us
  Pallas kernels  112 us (90%)
  local copies, waits for them, and re-layouts  6.07 us (5%)
  other arithmetic  1.62 us (1%)
  between operations  1.41 us (1%)
    pallas_call x1, Pallas kernels, main(): pl.pallas_call(functools.partial(main_kernel, n, cap, chunk), in_specs=[s...  108 us
    unnamed x18, local copies, waits for them, and re-layouts  3.78 us

profile of v5, /device:TPU:15, one launch (start us, length us, event | category | flops | bytes accessed | tf_op | source)
XLA Modules:
  0.0 121.4 jit_solution(13138284961248873081)
XLA Ops:
  0.6 0.0 copy-start.7
  0.6 0.0 copy-start.5
  0.7 0.0 copy-start.4
  1.3 0.8 reduce
  2.2 0.8 maximum_bitcast_fusion.q_ref
  3.0 0.0 copy-start
  3.0 1.2 %copy-done = bf16[512,1024]{1,0:T(8,128)(2,1)S(1)} copy-done((bf16[512,1024]{1,0:T(8,128)(2,1)S(1)}, bf16[512,1024]{1,0:T(8,128)(2,1)}, u32[]{:S(2)}) %copy-start) | copy-done | bytes 1048600
  4.2 0.0 copy-start.2
  4.2 1.2 %copy-done.2 = bf16[512,1024]{1,0:T(8,128)(2,1)S(1)} copy-done((bf16[512,1024]{1,0:T(8,128)(2,1)S(1)}, bf16[512,1024]{1,0:T(8,128)(2,1)}, u32[]{:S(2)}) %copy-start.2) | copy-done | bytes 1048600
  5.4 0.0 copy-start.6
  5.4 0.7 copy-done.6
  6.1 0.0 copy-start.8
  6.1 0.7 copy-done.8
  6.7 0.0 copy-start.1
  6.7 0.0 copy-start.3
  6.7 2.4 %pack.1 = (bf16[128,8,1024]{2,1,0:T(8,128)(2,1)S(1)}, bf16[128,8,1024]{2,1,0:T(8,128)(2,1)S(1)}, s32[16,8,128]{2,1,0:T(8,128)S(1)}) custom-call(s32[64]{0:T(128)S(1)} %bitcast.36, s32[16]{0:T(128)S(1)} %copy-done.6, s32[1]{0:T(128)S(6)} %copy.26.context, bf16[64,8,1024]{2,1,0:T(8,128)(2,1)S(1)} %bitcast.30, bf16[64,8,1024]{2,1,0:T(8,128)(2,1)S(1)} %bitcast.31), custom_call_target="tpu_custom_call" | custom-call | tf_op jit(solution)/shard_map/pack/pallas_call | solution.py:84
  9.1 0.0 copy-done.7
  9.2 0.0 copy-done.5
  9.2 0.0 copy-done.4
  9.2 0.0 copy-done.1
  9.2 0.0 copy-done.3
  9.2 107.8 %exchange.1 = (bf16[8,24,128]{2,1,0:T(8,128)(2,1)S(1)}, bf16[128,8,1024]{2,1,0:T(8,128)(2,1)S(1)}, bf16[128,8,1024]{2,1,0:T(8,128)(2,1)S(1)}, s32[16,8,128]{2,1,0:T(8,128)S(1)}) custom-call(s32[16]{0:T(128)S(1)} %copy-done.7, bf16[8,24,128]{2,1,0:T(8,128)(2,1)S(1)} %maximum_bitcast_fusion.q_ref, s32[16,8,128]{2,1,0:T(8,128)S(1)} %get-tuple-element.18.meta_ref, ...), custom_call_target="tpu_custom_call" | custom-call | tf_op jit(solution)/shard_map/exchange/pallas_call | solution.py:404
  117.1 2.0 %write.1 = (bf16[128,8,1024]{2,1,0:T(8,128)(2,1)}, bf16[128,8,1024]{2,1,0:T(8,128)(2,1)}) custom-call(bf16[128,8,1024]{2,1,0:T(8,128)(2,1)S(1)} %get-tuple-element.21.k_in, bf16[128,8,1024]{2,1,0:T(8,128)(2,1)S(1)} %get-tuple-element.22.v_in), custom_call_target="tpu_custom_call" | custom-call | tf_op jit(solution)/shard_map/write/pallas_call | solution.py:449
  119.1 0.4 slice_reduce_fusion
  119.5 0.6 reshape_squeeze.3
  120.1 0.6 reshape.43
  120.8 0.6 slice.14
  (3 shorter events, 0.0 us)
Async XLA Ops:
  0.6 8.5 %copy-start.7 = (s32[16]{0:T(128)S(1)}, s32[16]{0:T(128)}, u32[]{:S(2)}) copy-start(s32[16]{0:T(128)} %counts.3) | copy-start | bytes 196
  0.6 8.5 %copy-start.5 = (bf16[1,2,1024]{2,1,0:T(2,128)(2,1)S(1)}, bf16[1,2,1024]{2,1,0:T(2,128)(2,1)}, u32[]{:S(2)}) copy-start(bf16[1,2,1024]{2,1,0:T(2,128)(2,1)} %param.16) | copy-start | bytes 12292
  0.7 8.5 %copy-start.4 = (bf16[1,2,1024]{2,1,0:T(2,128)(2,1)S(1)}, bf16[1,2,1024]{2,1,0:T(2,128)(2,1)}, u32[]{:S(2)}) copy-start(bf16[1,2,1024]{2,1,0:T(2,128)(2,1)} %param.15) | copy-start | bytes 12292
  3.0 1.2 %copy-start = (bf16[512,1024]{1,0:T(8,128)(2,1)S(1)}, bf16[512,1024]{1,0:T(8,128)(2,1)}, u32[]{:S(2)}) copy-start(bf16[512,1024]{1,0:T(8,128)(2,1)} %ck_ref.1) | copy-start | bytes 3145732
  4.2 1.2 %copy-start.2 = (bf16[512,1024]{1,0:T(8,128)(2,1)S(1)}, bf16[512,1024]{1,0:T(8,128)(2,1)}, u32[]{:S(2)}) copy-start(bf16[512,1024]{1,0:T(8,128)(2,1)} %cv_ref.1) | copy-start | bytes 3145732
  5.4 0.7 copy-start.6
  6.1 0.7 copy-start.8
  6.7 2.5 %copy-start.1 = (bf16[512,1024]{1,0:T(8,128)(2,1)S(1)}, bf16[512,1024]{1,0:T(8,128)(2,1)}, u32[]{:S(2)}) copy-start(bf16[512,1024]{1,0:T(8,128)(2,1)} %ck_ref.1) | copy-start | bytes 3145732
  6.7 2.5 %copy-start.3 = (bf16[512,1024]{1,0:T(8,128)(2,1)S(1)}, bf16[512,1024]{1,0:T(8,128)(2,1)}, u32[]{:S(2)}) copy-start(bf16[512,1024]{1,0:T(8,128)(2,1)} %cv_ref.1) | copy-start | bytes 3145732
